TPU v7x, 32 devices: a whole 2x2x4 slice. The times are simulated.
32 devices in a mesh: ctx: 8 (over z, x), wsh: 4 (over y, core).
Axes of the slice: x: 2, y: 2, z: 4, core: 2. Of those that a mesh axis runs over, the one named last changes fastest.
Arguments:
- inputs: bfloat16 [8, 1024, 768], P('wsh', 'ctx'), may hold values from -6 to 6
- teacher: bfloat16 [8, 1024, 768], P('wsh', 'ctx'), may hold values from -6 to 6
- seq_lengths: int32 [8], P('wsh'), may hold values from 256 to 1024, as said below
- gain_attn: bfloat16 [768], P('wsh'), may hold values from 0.5 to 1.5
- w_query: bfloat16 [768, 768], P('wsh'), may hold values from -0.109375 to 0.109375
- w_key: bfloat16 [768, 768], P('wsh'), may hold values from -0.109375 to 0.109375
- w_value: bfloat16 [768, 768], P('wsh'), may hold values from -0.21875 to 0.21875
- w_out: bfloat16 [768, 768], P('wsh'), may hold values from -2.5 to 2.5
- bias_table: bfloat16 [32, 12], P('wsh'), may hold values from -4 to 4
- gain_ffn: bfloat16 [768], P('wsh'), may hold values from 0.5 to 1.5
- w_inner: bfloat16 [768, 3072], P('wsh'), may hold values from -0.21875 to 0.21875
- w_outer: bfloat16 [3072, 768], P('wsh'), may hold values from -0.109375 to 0.109375
Outputs:
- layer_out: bfloat16 [8, 1024, 768], P('wsh', 'ctx')
- loss_value: float32 [], replicated
- input_grad: float32 [8, 1024, 768], P('wsh', 'ctx')
- gain_attn_grad: float32 [768], P('wsh')
- w_query_grad: float32 [768, 768], P('wsh')
- w_key_grad: float32 [768, 768], P('wsh')
- w_value_grad: float32 [768, 768], P('wsh')
- w_out_grad: float32 [768, 768], P('wsh')
- bias_table_grad: float32 [32, 12], P('wsh')
- gain_ffn_grad: float32 [768], P('wsh')
- w_inner_grad: float32 [768, 3072], P('wsh')
- w_outer_grad: float32 [3072, 768], P('wsh')
Inputs may be any that keep to these rules, and one draw needn't show every extreme that they name: `seq_lengths`: in each aligned group of 2 sequences exactly one, chosen by the seed, has all 1024 tokens valid; every other sequence has fewer.
All inputs are finite; a program needn't handle non-finite values.
Results may differ from a plain program's by a relative error of at most 0.017.
Values may be sent and summed in bfloat16 or wider, within the bound.
No kernel may reach another device: no remote copies, remote signals or barrier semaphores. Data moves between devices by JAX's collectives and lax.ppermute only.
A program may use at most 128 MiB of HBM per device.

v0:
```python
import jax
import jax.numpy as jnp
from jax import lax
from jax.sharding import PartitionSpec as P

D = 768
H = 12
DH = 64
BUCKETS = 32
SEQ_DEV = 2
PIECE = 128
EPS = 1e-06
NEG_FILL = -1e30
BUCKET_EDGES = (12, 16, 23, 32, 46, 64, 91)


def passed_along(block, axis, distance):
    devices = range(lax.axis_size(axis))
    route = [((i - distance) % len(devices), i) for i in devices]
    return lax.ppermute(block, axis, route)


def for_sending(value):

    def short(part):
        return part.astype(jnp.bfloat16) if part.dtype == jnp.float32 else part

    return jax.tree.map(short, value)


def bucket_index(offset):
    distance = jnp.abs(offset)
    far_bucket = 8 + sum(((distance >= edge).astype(jnp.int32) for edge in BUCKET_EDGES))
    near_or_far = jnp.where(distance < 8, distance, far_bucket)
    return near_or_far + jnp.where(offset > 0, 16, 0)


def rms_scale(values, gain_vector):
    return values * lax.rsqrt(jnp.mean(values * values, axis=-1, keepdims=True) + EPS) * gain_vector


def gelu_exact(values):
    return jax.nn.gelu(values, approximate=False)


def rows_product(left, right):
    return lax.dot_general(
        left, right, (((0,), (0,)), ((), ())), preferred_element_type=jnp.float32
    )


def times_transposed(left, right):
    return lax.dot_general(
        left, right, (((1,), (1,)), ((), ())), preferred_element_type=jnp.float32
    )


def move_keys(blocks):
    return (passed_along(blocks[0], "ctx", 1),)


def move_grads(blocks):
    return (passed_along(for_sending(blocks[0]), "ctx", 1),)


def on_device(
    inputs,
    teacher,
    seq_lengths,
    gain_attn,
    w_query,
    w_key,
    w_value,
    w_out,
    bias_table,
    gain_ffn,
    w_inner,
    w_outer,
):
    cycle_size = lax.axis_size("ctx")
    cycle_pos = lax.axis_index("ctx")
    token_total = SEQ_DEV * PIECE * cycle_size * lax.axis_size("wsh")
    row_count = SEQ_DEV * PIECE
    shards = (gain_attn, w_query, w_key, w_value, w_out, bias_table, gain_ffn, w_inner, w_outer)
    gathered = (
        lax.all_gather(shards[0], "wsh", axis=0, tiled=True),
        lax.all_gather(shards[1], "wsh", axis=0, tiled=True),
        lax.all_gather(shards[2], "wsh", axis=0, tiled=True),
        lax.all_gather(shards[3], "wsh", axis=0, tiled=True),
        lax.all_gather(shards[4], "wsh", axis=0, tiled=True),
        lax.all_gather(shards[5], "wsh", axis=0, tiled=True),
        lax.all_gather(shards[6], "wsh", axis=0, tiled=True),
        lax.all_gather(shards[7], "wsh", axis=0, tiled=True),
        lax.all_gather(shards[8], "wsh", axis=0, tiled=True),
    )
    (
        attn_gain,
        query_full,
        key_full,
        value_full,
        out_full,
        table_full,
        ffn_gain,
        inner_full,
        outer_full,
    ) = gathered
    lane_plans = ((0, H, 1),)
    x_rows = inputs.reshape(row_count, D).astype(jnp.float32)
    normed, attn_norm_back = jax.vjp(rms_scale, x_rows, attn_gain.astype(jnp.float32))
    normed_low = normed.astype(jnp.bfloat16)
    query_low = jnp.dot(normed_low, query_full, preferred_element_type=jnp.float32).astype(
        jnp.bfloat16
    )
    key_low = jnp.dot(normed_low, key_full, preferred_element_type=jnp.float32).astype(jnp.bfloat16)
    value_low = jnp.dot(normed_low, value_full, preferred_element_type=jnp.float32).astype(
        jnp.bfloat16
    )
    query_heads = query_low.reshape(SEQ_DEV, PIECE, H, DH)
    key_value = jnp.stack([key_low, value_low]).reshape(2, SEQ_DEV, PIECE, H * DH)
    places = jnp.arange(PIECE, dtype=jnp.int32)
    query_places = cycle_pos * PIECE + places
    bucket_ids = jnp.arange(BUCKETS, dtype=jnp.int32)

    def lane_blocks(stacked):
        return tuple((stacked for plan in lane_plans))

    def lane_scores(lane_plan, query_part, lane_block, key_start, table_rows):
        head_count = lane_plan[1] - lane_plan[0]
        key_count = lane_block.shape[2]
        key_places = key_start + jnp.arange(key_count, dtype=jnp.int32)
        offset = (key_places[None, :] - query_places[:, None]).reshape(-1)
        onehot = (bucket_index(offset)[None, :] == bucket_ids[:, None]).astype(jnp.bfloat16)
        bias_rows = jnp.dot(table_rows, onehot, preferred_element_type=jnp.float32)
        key_part = lane_block[0].reshape(SEQ_DEV, key_count, head_count, DH)
        scores = jnp.einsum(
            "sihd,sjhd->shij", query_part, key_part, preferred_element_type=jnp.float32
        )
        scores = scores + bias_rows.reshape(head_count, PIECE, key_count)[None]
        key_ok = key_places[None, :] < seq_lengths[:, None]
        return (jnp.where(key_ok[:, None, None, :], scores, NEG_FILL), onehot)

    table_forward = table_full.T

    def absorb(lane_plan, lane_state, lane_block, key_start):
        head_count = lane_plan[1] - lane_plan[0]
        key_count = lane_block.shape[2]
        row_max, row_total, accum = lane_state
        scores, onehot = lane_scores(lane_plan, query_heads, lane_block, key_start, table_forward)
        new_max = jnp.maximum(row_max, jnp.max(scores, axis=-1))
        rescale = jnp.exp(row_max - new_max)
        weights = jnp.exp(scores - new_max[..., None])
        row_total = row_total * rescale + jnp.sum(weights, axis=-1)
        value_part = lane_block[1].reshape(SEQ_DEV, key_count, head_count, DH)
        update = jnp.einsum(
            "shij,sjhd->sihd",
            weights.astype(jnp.bfloat16),
            value_part,
            preferred_element_type=jnp.float32,
        )
        accum = accum * jnp.transpose(rescale, (0, 2, 1))[..., None] + update
        return (new_max, row_total, accum)

    def empty_state(plan):
        head_count = plan[1] - plan[0]
        return (
            jnp.full((SEQ_DEV, head_count, PIECE), NEG_FILL, jnp.float32),
            jnp.zeros((SEQ_DEV, head_count, PIECE), jnp.float32),
            jnp.zeros((SEQ_DEV, PIECE, head_count, DH), jnp.float32),
        )

    def empty_accum(plan):
        head_count = plan[1] - plan[0]
        return (
            jnp.zeros((SEQ_DEV, PIECE, head_count, DH), jnp.float32),
            jnp.zeros((head_count, BUCKETS), jnp.float32),
        )

    blocks = lane_blocks(key_value)
    states = tuple(
        (
            absorb(plan, empty_state(plan), lane_block, cycle_pos * PIECE)
            for plan, lane_block in zip(lane_plans, blocks)
        )
    )

    def forward_turn(turn_index, loop_carry):
        arrived = move_keys(loop_carry[0])
        new_states = tuple(
            (
                absorb(
                    plan,
                    lane_state,
                    lane_block,
                    (cycle_pos - plan[2] * turn_index) % cycle_size * PIECE,
                )
                for plan, lane_state, lane_block in zip(lane_plans, loop_carry[1], arrived)
            )
        )
        return (arrived, new_states)

    blocks, states = lax.fori_loop(1, cycle_size, forward_turn, (blocks, states))
    log_totals = jnp.concatenate(
        [lane_state[0] + jnp.log(lane_state[1]) for lane_state in states], axis=1
    )
    attn_out = jnp.concatenate(
        [
            lane_state[2] / jnp.transpose(lane_state[1], (0, 2, 1))[..., None]
            for lane_state in states
        ],
        axis=2,
    )
    attn_low = attn_out.reshape(row_count, H * DH).astype(jnp.bfloat16)
    hidden = x_rows + jnp.dot(attn_low, out_full, preferred_element_type=jnp.float32)
    normed_ffn, ffn_norm_back = jax.vjp(rms_scale, hidden, ffn_gain.astype(jnp.float32))
    ffn_low = normed_ffn.astype(jnp.bfloat16)
    inner_sum = jnp.dot(ffn_low, inner_full, preferred_element_type=jnp.float32)
    active, gelu_back = jax.vjp(gelu_exact, inner_sum)
    active_low = active.astype(jnp.bfloat16)
    result = hidden + jnp.dot(active_low, outer_full, preferred_element_type=jnp.float32)
    row_valid = (
        (query_places[None, :] < seq_lengths[:, None]).astype(jnp.float32).reshape(row_count, 1)
    )
    deviation = result - teacher.reshape(row_count, D).astype(jnp.float32)
    square_sum, valid_count = lax.psum(
        (jnp.sum(deviation * deviation * row_valid), jnp.sum(row_valid)), ("ctx", "wsh")
    )
    loss_value = square_sum / (valid_count * D)
    result_grad = token_total / valid_count * deviation * row_valid
    result_low = result_grad.astype(jnp.bfloat16)
    query_back = gathered[1]
    key_back = gathered[2]
    value_back = gathered[3]
    out_back = gathered[4]
    table_back = gathered[5].T
    inner_back = gathered[7]
    outer_back = gathered[8]
    outer_grad = rows_product(active_low, result_low)
    active_grad = times_transposed(result_low, outer_back)
    inner_grad = gelu_back(active_grad)[0].astype(jnp.bfloat16)
    inner_wgrad = rows_product(ffn_low, inner_grad)
    ffn_normed_grad = times_transposed(inner_grad, inner_back)
    hidden_part, ffn_gain_grad = ffn_norm_back(ffn_normed_grad)
    hidden_grad = result_grad + hidden_part
    hidden_low = hidden_grad.astype(jnp.bfloat16)
    out_wgrad = rows_product(attn_low, hidden_low)
    dout_heads = (
        times_transposed(hidden_low, out_back).astype(jnp.bfloat16).reshape(SEQ_DEV, PIECE, H, DH)
    )
    out_dot = jnp.transpose(jnp.sum(dout_heads.astype(jnp.float32) * attn_out, axis=-1), (0, 2, 1))

    def lane_back(lane_plan, lane_block, lane_accum, key_start):
        low_head, high_head = (lane_plan[0], lane_plan[1])
        head_count = high_head - low_head
        key_count = lane_block.shape[2]
        scores, onehot = lane_scores(lane_plan, query_heads, lane_block, key_start, table_back)
        probability = jnp.exp(scores - log_totals[:, low_head:high_head, :, None])
        prob_low = probability.astype(jnp.bfloat16)
        key_part = lane_block[0].reshape(SEQ_DEV, key_count, head_count, DH)
        value_part = lane_block[1].reshape(SEQ_DEV, key_count, head_count, DH)
        value_grad = jnp.einsum(
            "shij,sihd->sjhd", prob_low, dout_heads, preferred_element_type=jnp.float32
        )
        prob_grad = jnp.einsum(
            "sihd,sjhd->shij", dout_heads, value_part, preferred_element_type=jnp.float32
        )
        score_grad = (probability * (prob_grad - out_dot[:, low_head:high_head, :, None])).astype(
            jnp.bfloat16
        )
        query_grad = lane_accum[0] + jnp.einsum(
            "shij,sjhd->sihd", score_grad, key_part, preferred_element_type=jnp.float32
        )
        key_grad = jnp.einsum(
            "shij,sihd->sjhd", score_grad, query_heads, preferred_element_type=jnp.float32
        )
        table_grad = lane_accum[1] + jnp.einsum(
            "shk,bk->hb",
            score_grad.reshape(SEQ_DEV, head_count, PIECE * key_count),
            onehot,
            preferred_element_type=jnp.float32,
        )
        term = jnp.stack([key_grad, value_grad]).reshape(2, SEQ_DEV, key_count, head_count * DH)
        return (term, (query_grad, table_grad))

    blocks = lane_blocks(key_value)
    outcome = [
        lane_back(plan, lane_block, empty_accum(plan), cycle_pos * PIECE)
        for plan, lane_block in zip(lane_plans, blocks)
    ]
    grad_blocks = move_grads(tuple((entry[0] for entry in outcome)))
    accums = tuple((entry[1] for entry in outcome))

    def back_turn(turn_index, loop_carry):
        arrived = move_keys(loop_carry[0])
        outcome = [
            lane_back(
                plan,
                lane_block,
                lane_accum,
                (cycle_pos - plan[2] * turn_index) % cycle_size * PIECE,
            )
            for plan, lane_block, lane_accum in zip(lane_plans, arrived, loop_carry[2])
        ]
        new_grads = move_grads(
            tuple((grad_block + entry[0] for grad_block, entry in zip(loop_carry[1], outcome)))
        )
        return (arrived, new_grads, tuple((entry[1] for entry in outcome)))

    blocks, grad_blocks, accums = lax.fori_loop(
        1, cycle_size, back_turn, (blocks, grad_blocks, accums)
    )
    pair_grads = grad_blocks[0]
    query_grad_low = (
        jnp.concatenate([lane_accum[0] for lane_accum in accums], axis=2)
        .reshape(row_count, H * DH)
        .astype(jnp.bfloat16)
    )
    key_grad_low = pair_grads[0].reshape(row_count, H * DH).astype(jnp.bfloat16)
    value_grad_low = pair_grads[1].reshape(row_count, H * DH).astype(jnp.bfloat16)
    table_grad = jnp.concatenate([lane_accum[1] for lane_accum in accums], axis=0).T
    query_wgrad = rows_product(normed_low, query_grad_low)
    key_wgrad = rows_product(normed_low, key_grad_low)
    value_wgrad = rows_product(normed_low, value_grad_low)
    normed_grad = (
        times_transposed(query_grad_low, query_back)
        + times_transposed(key_grad_low, key_back)
        + times_transposed(value_grad_low, value_back)
    )
    input_part, attn_gain_grad = attn_norm_back(normed_grad)
    input_grad = hidden_grad + input_part
    local_grads = (
        attn_gain_grad,
        query_wgrad,
        key_wgrad,
        value_wgrad,
        out_wgrad,
        table_grad,
        ffn_gain_grad,
        inner_wgrad,
        outer_grad,
    )
    shares = (
        lax.psum_scatter(
            local_grads[0].astype(jnp.bfloat16), "wsh", scatter_dimension=0, tiled=True
        ).astype(jnp.float32),
        lax.psum_scatter(
            local_grads[1].astype(jnp.bfloat16), "wsh", scatter_dimension=0, tiled=True
        ).astype(jnp.float32),
        lax.psum_scatter(
            local_grads[2].astype(jnp.bfloat16), "wsh", scatter_dimension=0, tiled=True
        ).astype(jnp.float32),
        lax.psum_scatter(
            local_grads[3].astype(jnp.bfloat16), "wsh", scatter_dimension=0, tiled=True
        ).astype(jnp.float32),
        lax.psum_scatter(
            local_grads[4].astype(jnp.bfloat16), "wsh", scatter_dimension=0, tiled=True
        ).astype(jnp.float32),
        lax.psum_scatter(
            local_grads[5].astype(jnp.bfloat16), "wsh", scatter_dimension=0, tiled=True
        ).astype(jnp.float32),
        lax.psum_scatter(
            local_grads[6].astype(jnp.bfloat16), "wsh", scatter_dimension=0, tiled=True
        ).astype(jnp.float32),
        lax.psum_scatter(
            local_grads[7].astype(jnp.bfloat16), "wsh", scatter_dimension=0, tiled=True
        ).astype(jnp.float32),
        lax.psum_scatter(
            local_grads[8].astype(jnp.bfloat16), "wsh", scatter_dimension=0, tiled=True
        ).astype(jnp.float32),
    )
    totals = lax.psum(
        (
            shares[0],
            shares[1],
            shares[2],
            shares[3],
            shares[4],
            shares[5],
            shares[6],
            shares[7],
            shares[8],
        ),
        "ctx",
    )
    return (
        result.reshape(SEQ_DEV, PIECE, D).astype(jnp.bfloat16),
        loss_value,
        input_grad.reshape(SEQ_DEV, PIECE, D),
        totals[0],
        totals[1],
        totals[2],
        totals[3],
        totals[4],
        totals[5],
        totals[6],
        totals[7],
        totals[8],
    )


def solution(mesh):
    placed = (
        P("wsh", "ctx", None),
        P("wsh", "ctx", None),
        P("wsh"),
        P("wsh"),
        P("wsh", None),
        P("wsh", None),
        P("wsh", None),
        P("wsh", None),
        P("wsh", None),
        P("wsh"),
        P("wsh", None),
        P("wsh", None),
    )
    return jax.shard_map(
        on_device,
        mesh=mesh,
        in_specs=placed,
        out_specs=(
            P("wsh", "ctx", None),
            P(),
            P("wsh", "ctx", None),
            P("wsh"),
            P("wsh", None),
            P("wsh", None),
            P("wsh", None),
            P("wsh", None),
            P("wsh", None),
            P("wsh"),
            P("wsh", None),
            P("wsh", None),
        ),
        check_vma=False,
    )
```

profile of v0, /device:TPU:0, one launch (start us, length us, event | category | flops | bytes accessed | tf_op | source)
XLA Modules:
  0.0 1081.6 jit_solution(2276786720739246816)
XLA Ops:
  13.8 8.4 all-reduce.8
  22.3 5.2 all_gather.31
  33.1 1.7 convolution_convert_fusion.9
  35.1 14.0 %all-gather.7.cloned.1.call-done = bf16[768,768]{1,0:T(8,128)(2,1)} async-done(((bf16[192,768]{1,0:T(8,128)(2,1)}), bf16[768,768]{1,0:T(8,128)(2,1)}) %all-gather.7.cloned.1.call-update) | async-done | bytes 1179664 | tf_op jit(solution)/shard_map/all_gather | solution.py:88
  49.1 1.7 convolution_convert_fusion.11
  51.2 1.7 fusion.112
  54.1 14.0 %all-gather.9.cloned.1.call-done = bf16[768,768]{1,0:T(8,128)(2,1)} async-done(((bf16[192,768]{1,0:T(8,128)(2,1)}), bf16[768,768]{1,0:T(8,128)(2,1)}) %all-gather.9.cloned.1.call-update) | async-done | bytes 1179664 | tf_op jit(solution)/shard_map/all_gather | solution.py:89
  68.1 1.7 convolution_convert_fusion.10
  72.0 155.8 %while.44 = (s32[]{:T(128)}, bf16[2,2,128,768]{2,3,1,0:T(8,128)(2,1)}, f32[2,12,128]{2,1,0:T(8,128)S(1)}, f32[2,12,128]{2,1,0:T(8,128)}, f32[2,128,12,64]{1,3,2,...) while((s32[]{:T(128)}, ...), condition=%wide.region_6.7_spmd.clone, body=%wide.region_3.6_spmd.clone.sunk | while | flops 117384720 | bytes 21013696 | solution.py:201
  75.9 19.2 %collective-permute-done = bf16[2,2,128,768]{2,3,1,0:T(8,128)(2,1)S(1)} collective-permute-done((bf16[2,2,128,768]{2,3,1,0:T(8,128)(2,1)}, bf16[2,2,128,768]{2,3,1,0:T(8,128)(2,1)S(1)}, u32[]{:S(2)}, u32[]{:S(2)}) %collective-permute-start) | collective-permute-done | bytes 786464 | tf_op jit(solution)/shard_map/while/body/eval_jaxpr/ppermute | solution.py:20
  99.3 19.9 %collective-permute-done = bf16[2,2,128,768]{2,3,1,0:T(8,128)(2,1)S(1)} collective-permute-done((bf16[2,2,128,768]{2,3,1,0:T(8,128)(2,1)}, bf16[2,2,128,768]{2,3,1,0:T(8,128)(2,1)S(1)}, u32[]{:S(2)}, u32[]{:S(2)}) %collective-permute-start) | collective-permute-done | bytes 786464 | tf_op jit(solution)/shard_map/while/body/eval_jaxpr/ppermute | solution.py:20
  123.3 18.9 %collective-permute-done = bf16[2,2,128,768]{2,3,1,0:T(8,128)(2,1)S(1)} collective-permute-done((bf16[2,2,128,768]{2,3,1,0:T(8,128)(2,1)}, bf16[2,2,128,768]{2,3,1,0:T(8,128)(2,1)S(1)}, u32[]{:S(2)}, u32[]{:S(2)}) %collective-permute-start) | collective-permute-done | bytes 786464 | tf_op jit(solution)/shard_map/while/body/eval_jaxpr/ppermute | solution.py:20
  146.5 18.0 %collective-permute-done = bf16[2,2,128,768]{2,3,1,0:T(8,128)(2,1)S(1)} collective-permute-done((bf16[2,2,128,768]{2,3,1,0:T(8,128)(2,1)}, bf16[2,2,128,768]{2,3,1,0:T(8,128)(2,1)S(1)}, u32[]{:S(2)}, u32[]{:S(2)}) %collective-permute-start) | collective-permute-done | bytes 786464 | tf_op jit(solution)/shard_map/while/body/eval_jaxpr/ppermute | solution.py:20
  168.6 17.1 %collective-permute-done = bf16[2,2,128,768]{2,3,1,0:T(8,128)(2,1)S(1)} collective-permute-done((bf16[2,2,128,768]{2,3,1,0:T(8,128)(2,1)}, bf16[2,2,128,768]{2,3,1,0:T(8,128)(2,1)S(1)}, u32[]{:S(2)}, u32[]{:S(2)}) %collective-permute-start) | collective-permute-done | bytes 786464 | tf_op jit(solution)/shard_map/while/body/eval_jaxpr/ppermute | solution.py:20
  189.9 16.2 %collective-permute-done = bf16[2,2,128,768]{2,3,1,0:T(8,128)(2,1)S(1)} collective-permute-done((bf16[2,2,128,768]{2,3,1,0:T(8,128)(2,1)}, bf16[2,2,128,768]{2,3,1,0:T(8,128)(2,1)S(1)}, u32[]{:S(2)}, u32[]{:S(2)}) %collective-permute-start) | collective-permute-done | bytes 786464 | tf_op jit(solution)/shard_map/while/body/eval_jaxpr/ppermute | solution.py:20
  210.3 15.2 %collective-permute-done = bf16[2,2,128,768]{2,3,1,0:T(8,128)(2,1)S(1)} collective-permute-done((bf16[2,2,128,768]{2,3,1,0:T(8,128)(2,1)}, bf16[2,2,128,768]{2,3,1,0:T(8,128)(2,1)S(1)}, u32[]{:S(2)}, u32[]{:S(2)}) %collective-permute-start) | collective-permute-done | bytes 786464 | tf_op jit(solution)/shard_map/while/body/eval_jaxpr/ppermute | solution.py:20
  230.2 2.1 multiply_reduce_fusion.4
  233.1 11.2 %multiply_convert_fusion.1 = (bf16[256,3072]{1,0:T(8,128)(2,1)S(1)}, f32[256,3072]{1,0:T(8,128)}, f32[256,3072]{1,0:T(8,128)}) fusion(bf16[768,3072]{1,0:T(8,128)(2,1)} %all-gather.15.cloned.1.call-done, f32[256,768]{1,0:T(8,128)S(1)} %get-tuple-element.884, f32[768]{0:T(1024)S(1)} %copy-done.42, f32[256]{0:T(256)S(1)} %fusion.98), kind=kOutput, calls=%fused_computation.67 | convolution fusion | flops 1259667456 | bytes 13373440 | tf_op jit(solution)/shard_map/dot_general | solution.py:216
  244.3 5.0 multiply_reduce_fusion.3
  249.3 37.3 %all-reduce.5 = (f32[]{:T(128)}, f32[]{:T(128)}) all-reduce(f32[]{:T(128)} %get-tuple-element.886, f32[]{:T(128)} %get-tuple-element.855), channel_id=1, replica_groups=mesh['ctx'=8,'wsh'=4] {'ctx','wsh'}, use_global_device_ids=true, to_apply=%region_9.10 | all-reduce | flops 2 | bytes 16 | tf_op jit(solution)/shard_map/psum | solution.py:224
  288.6 6.4 add_convert_fusion
  295.1 2.1 multiply_reduce_fusion
  297.3 2.5 fusion.57
  307.9 2.3 collective-permute-start.3
  314.9 14.6 %collective-permute-done.3 = bf16[2,2,128,768]{2,3,1,0:T(8,128)(2,1)S(1)} collective-permute-done((bf16[2,2,128,768]{2,3,1,0:T(8,128)(2,1)}, bf16[2,2,128,768]{2,3,1,0:T(8,128)(2,1)S(1)}, u32[]{:S(2)}, u32[]{:S(2)}) %collective-permute-start.3) | collective-permute-done | bytes 786464 | tf_op jit(solution)/shard_map/ppermute | solution.py:20
  329.5 279.1 %while.45 = (s32[]{:T(128)}, bf16[2,2,128,768]{2,3,1,0:T(8,128)(2,1)}, bf16[2,2,128,768]{2,3,1,0:T(8,128)(2,1)S(1)}, f32[2,128,12,64]{1,3,2,0:T(8,128)S(1)}, f32...) while((s32[]{:T(128)}, ...), condition=%wide.region_17.18_spmd.clone, body=%wide.region_15.17_spmd.clone.sunk | while | flops 283444096 | bytes 33844516 | solution.py:308
  331.4 19.0 %collective-permute-done.1 = bf16[2,2,128,768]{2,3,1,0:T(8,128)(2,1)S(1)} collective-permute-done((bf16[2,2,128,768]{2,3,1,0:T(8,128)(2,1)}, bf16[2,2,128,768]{2,3,1,0:T(8,128)(2,1)S(1)}, u32[]{:S(2)}, u32[]{:S(2)}) %collective-permute-start.1) | collective-permute-done | bytes 786464 | tf_op jit(solution)/shard_map/while/body/eval_jaxpr/ppermute | solution.py:20
  355.4 17.0 %collective-permute-done.2 = bf16[2,2,128,768]{2,3,1,0:T(8,128)(2,1)S(1)} collective-permute-done((bf16[2,2,128,768]{2,3,1,0:T(8,128)(2,1)S(1)}, bf16[2,2,128,768]{2,3,1,0:T(8,128)(2,1)S(1)}, u32[]{:S(2)}, u32[]{:S(2)}) %collective-permute-start.2) | collective-permute-done | bytes 786464 | tf_op jit(solution)/shard_map/while/body/eval_jaxpr/ppermute | solution.py:20
  374.1 17.2 %collective-permute-done.1 = bf16[2,2,128,768]{2,3,1,0:T(8,128)(2,1)S(1)} collective-permute-done((bf16[2,2,128,768]{2,3,1,0:T(8,128)(2,1)}, bf16[2,2,128,768]{2,3,1,0:T(8,128)(2,1)S(1)}, u32[]{:S(2)}, u32[]{:S(2)}) %collective-permute-start.1) | collective-permute-done | bytes 786464 | tf_op jit(solution)/shard_map/while/body/eval_jaxpr/ppermute | solution.py:20
  396.2 15.2 %collective-permute-done.2 = bf16[2,2,128,768]{2,3,1,0:T(8,128)(2,1)S(1)} collective-permute-done((bf16[2,2,128,768]{2,3,1,0:T(8,128)(2,1)S(1)}, bf16[2,2,128,768]{2,3,1,0:T(8,128)(2,1)S(1)}, u32[]{:S(2)}, u32[]{:S(2)}) %collective-permute-start.2) | collective-permute-done | bytes 786464 | tf_op jit(solution)/shard_map/while/body/eval_jaxpr/ppermute | solution.py:20
  413.1 15.3 %collective-permute-done.1 = bf16[2,2,128,768]{2,3,1,0:T(8,128)(2,1)S(1)} collective-permute-done((bf16[2,2,128,768]{2,3,1,0:T(8,128)(2,1)}, bf16[2,2,128,768]{2,3,1,0:T(8,128)(2,1)S(1)}, u32[]{:S(2)}, u32[]{:S(2)}) %collective-permute-start.1) | collective-permute-done | bytes 786464 | tf_op jit(solution)/shard_map/while/body/eval_jaxpr/ppermute | solution.py:20
  433.4 15.0 %collective-permute-done.2 = bf16[2,2,128,768]{2,3,1,0:T(8,128)(2,1)S(1)} collective-permute-done((bf16[2,2,128,768]{2,3,1,0:T(8,128)(2,1)S(1)}, bf16[2,2,128,768]{2,3,1,0:T(8,128)(2,1)S(1)}, u32[]{:S(2)}, u32[]{:S(2)}) %collective-permute-start.2) | collective-permute-done | bytes 786464 | tf_op jit(solution)/shard_map/while/body/eval_jaxpr/ppermute | solution.py:20
  450.0 13.8 %collective-permute-done.1 = bf16[2,2,128,768]{2,3,1,0:T(8,128)(2,1)S(1)} collective-permute-done((bf16[2,2,128,768]{2,3,1,0:T(8,128)(2,1)}, bf16[2,2,128,768]{2,3,1,0:T(8,128)(2,1)S(1)}, u32[]{:S(2)}, u32[]{:S(2)}) %collective-permute-start.1) | collective-permute-done | bytes 786464 | tf_op jit(solution)/shard_map/while/body/eval_jaxpr/ppermute | solution.py:20
  468.8 15.8 %collective-permute-done.2 = bf16[2,2,128,768]{2,3,1,0:T(8,128)(2,1)S(1)} collective-permute-done((bf16[2,2,128,768]{2,3,1,0:T(8,128)(2,1)S(1)}, bf16[2,2,128,768]{2,3,1,0:T(8,128)(2,1)S(1)}, u32[]{:S(2)}, u32[]{:S(2)}) %collective-permute-start.2) | collective-permute-done | bytes 786464 | tf_op jit(solution)/shard_map/while/body/eval_jaxpr/ppermute | solution.py:20
  486.3 15.6 %collective-permute-done.1 = bf16[2,2,128,768]{2,3,1,0:T(8,128)(2,1)S(1)} collective-permute-done((bf16[2,2,128,768]{2,3,1,0:T(8,128)(2,1)}, bf16[2,2,128,768]{2,3,1,0:T(8,128)(2,1)S(1)}, u32[]{:S(2)}, u32[]{:S(2)}) %collective-permute-start.1) | collective-permute-done | bytes 786464 | tf_op jit(solution)/shard_map/while/body/eval_jaxpr/ppermute | solution.py:20
  506.9 18.0 %collective-permute-done.2 = bf16[2,2,128,768]{2,3,1,0:T(8,128)(2,1)S(1)} collective-permute-done((bf16[2,2,128,768]{2,3,1,0:T(8,128)(2,1)S(1)}, bf16[2,2,128,768]{2,3,1,0:T(8,128)(2,1)S(1)}, u32[]{:S(2)}, u32[]{:S(2)}) %collective-permute-start.2) | collective-permute-done | bytes 786464 | tf_op jit(solution)/shard_map/while/body/eval_jaxpr/ppermute | solution.py:20
  526.5 17.8 %collective-permute-done.1 = bf16[2,2,128,768]{2,3,1,0:T(8,128)(2,1)S(1)} collective-permute-done((bf16[2,2,128,768]{2,3,1,0:T(8,128)(2,1)}, bf16[2,2,128,768]{2,3,1,0:T(8,128)(2,1)S(1)}, u32[]{:S(2)}, u32[]{:S(2)}) %collective-permute-start.1) | collective-permute-done | bytes 786464 | tf_op jit(solution)/shard_map/while/body/eval_jaxpr/ppermute | solution.py:20
  549.3 20.3 %collective-permute-done.2 = bf16[2,2,128,768]{2,3,1,0:T(8,128)(2,1)S(1)} collective-permute-done((bf16[2,2,128,768]{2,3,1,0:T(8,128)(2,1)S(1)}, bf16[2,2,128,768]{2,3,1,0:T(8,128)(2,1)S(1)}, u32[]{:S(2)}, u32[]{:S(2)}) %collective-permute-start.2) | collective-permute-done | bytes 786464 | tf_op jit(solution)/shard_map/while/body/eval_jaxpr/ppermute | solution.py:20
  571.3 20.1 %collective-permute-done.1 = bf16[2,2,128,768]{2,3,1,0:T(8,128)(2,1)S(1)} collective-permute-done((bf16[2,2,128,768]{2,3,1,0:T(8,128)(2,1)}, bf16[2,2,128,768]{2,3,1,0:T(8,128)(2,1)S(1)}, u32[]{:S(2)}, u32[]{:S(2)}) %collective-permute-start.1) | collective-permute-done | bytes 786464 | tf_op jit(solution)/shard_map/while/body/eval_jaxpr/ppermute | solution.py:20
  596.4 12.2 %collective-permute-done.2 = bf16[2,2,128,768]{2,3,1,0:T(8,128)(2,1)S(1)} collective-permute-done((bf16[2,2,128,768]{2,3,1,0:T(8,128)(2,1)S(1)}, bf16[2,2,128,768]{2,3,1,0:T(8,128)(2,1)S(1)}, u32[]{:S(2)}, u32[]{:S(2)}) %collective-permute-start.2) | collective-permute-done | bytes 786464 | tf_op jit(solution)/shard_map/while/body/eval_jaxpr/ppermute | solution.py:20
  615.1 5.2 convolution_convert_fusion.1
  621.7 3.6 convolution_convert_fusion
  631.2 11.3 %all-reduce.7 = (bf16[768]{0:T(1024)(128)(2,1)S(1)}, bf16[32,12]{1,0:T(8,128)(2,1)S(1)}, bf16[768]{0:T(1024)(128)(2,1)S(1)}) all-reduce(bf16[768]{0:T(1024)(128)(2,1)S(1)} %get-tuple-element.789, bf16[32,12]{1,0:T(8,128)(2,1)S(1)} %copy.186, bf16[768]{0:T(1024)(128)(2,1)S(1)} %copy-done.64), channel_id=2, replica_groups=mesh['ctx'=8,'wsh'=4] {'wsh'}, use_global_device_ids=true, to_apply=%region_20.21.clone | all-reduce | flops 1920 | bytes 7680
  643.6 21.0 %reduce-scatter.11.cloned.1.call-done = bf16[192,768]{1,0:T(8,128)(2,1)} async-done(((bf16[768,768]{1,0:T(8,128)(2,1)}), bf16[192,768]{1,0:T(8,128)(2,1)}) %reduce-scatter.11.cloned.1.call-update) | async-done | bytes 294928 | tf_op jit(solution)/shard_map/reduce_scatter | solution.py:351
  664.7 28.9 %reduce-scatter.7.cloned.1.call-done = bf16[192,768]{1,0:T(8,128)(2,1)} async-done(((bf16[768,768]{1,0:T(8,128)(2,1)}), bf16[192,768]{1,0:T(8,128)(2,1)}) %reduce-scatter.7.cloned.1.call-update) | async-done | bytes 294928 | tf_op jit(solution)/shard_map/reduce_scatter | solution.py:345
  693.6 50.4 %reduce-scatter.15.cloned.1.call-done = bf16[192,3072]{1,0:T(8,128)(2,1)} async-done(((bf16[768,3072]{1,0:T(8,128)(2,1)}), bf16[192,3072]{1,0:T(8,128)(2,1)}) %reduce-scatter.15.cloned.1.call-update) | async-done | bytes 1179664 | tf_op jit(solution)/shard_map/reduce_scatter | solution.py:363
  744.0 50.4 %reduce-scatter.17.cloned.1.call-done = bf16[768,768]{1,0:T(8,128)(2,1)} async-done(((bf16[3072,768]{1,0:T(8,128)(2,1)}), bf16[768,768]{1,0:T(8,128)(2,1)}) %reduce-scatter.17.cloned.1.call-update) | async-done | bytes 1179664 | tf_op jit(solution)/shard_map/reduce_scatter | solution.py:366
  794.4 279.1 %all-reduce.10 = (f32[192]{0:T(256)}, f32[192,768]{1,0:T(8,128)}, f32[192,768]{1,0:T(8,128)}, f32[192,768]{1,0:T(8,128)}, f32[192,768]{1,0:T(8,128)}, /*index=5*...) all-reduce(f32[192]{0:T(256)S(1)} %get-tuple-element.893, ...), channel_id=1, replica_groups=mesh['ctx'=8,'wsh'=4] {'ctx'}, use_global_device_ids=true, to_apply=%region_21.22 | all-reduce | flops 1769952 | bytes 10620672 | tf_op jit(solution)/shard_map/psum | solution.py:370
  (588 shorter events, 119.8 us)
Async XLA Ops:
  7.2 15.1 %copy-start.62 = (bf16[8,12]{1,0:T(8,128)(2,1)S(1)}, bf16[8,12]{1,0:T(8,128)(2,1)}, u32[]{:S(2)}) copy-start(bf16[8,12]{1,0:T(8,128)(2,1)} %param.24) | copy-start | bytes 580
  7.2 25.8 %all-gather.11.cloned.1.call-start = ((), (), s32[]{:S(2)}) async-start(), calls=%async_computation.8 | async-start | bytes 1474560 | tf_op jit(solution)/shard_map/all_gather | solution.py:87
  8.0 41.1 %all-gather.7.cloned.1.call-start = ((), (), s32[]{:S(2)}) async-start(), calls=%async_computation.6 | async-start | bytes 1474560 | tf_op jit(solution)/shard_map/all_gather | solution.py:88
  8.7 59.4 %all-gather.9.cloned.1.call-start = ((), (), s32[]{:S(2)}) async-start(), calls=%async_computation.7 | async-start | bytes 1474560 | tf_op jit(solution)/shard_map/all_gather | solution.py:89
  9.5 220.8 %all-gather.13.cloned.1.call-start = ((), (), s32[]{:S(2)}) async-start(), calls=%async_computation.9 | async-start | bytes 1474560 | tf_op jit(solution)/shard_map/all_gather | solution.py:90
  10.0 223.0 %all-gather.15.cloned.1.call-start = ((), (), s32[]{:S(2)}) async-start(), calls=%async_computation.10 | async-start | bytes 5898240 | tf_op jit(solution)/shard_map/all_gather | solution.py:93
  10.6 233.7 %all-gather.17.cloned.1.call-start = ((), (), s32[]{:S(2)}) async-start(), calls=%async_computation.11 | async-start | bytes 5898240 | tf_op jit(solution)/shard_map/all_gather | solution.py:94
  11.2 632.4 %reduce-scatter.13.cloned.1.call-start = ((), (), s32[]{:S(2)}) async-start(), calls=%async_computation.15 | async-start | bytes 1474560 | tf_op jit(solution)/shard_map/reduce_scatter | solution.py:354
  11.9 20.0 %copy-start.49 = (f32[256]{0:T(256)}, f32[256]{0:T(256)S(1)}, u32[]{:S(2)}) copy-start(f32[256]{0:T(256)S(1)} %bitcast_rsqrt_fusion) | copy-start | bytes 3076
  35.1 17.8 %copy-start.8 = (bf16[2,128,12,64]{1,0,3,2:T(2,128)(2,1)}, bf16[2,128,12,64]{1,0,3,2:T(2,128)(2,1)S(1)}, u32[]{:S(2)}) copy-start(bf16[2,128,12,64]{1,0,3,2:T(2,128)(2,1)S(1)} %reshape.466) | copy-start | bytes 1179652
  52.9 18.7 %copy-start = (f32[2,12,128,128]{2,3,1,0:T(8,128)}, f32[2,12,128,128]{2,3,1,0:T(8,128)S(1)}, u32[]{:S(2)}) copy-start(f32[2,12,128,128]{2,3,1,0:T(8,128)S(1)} %get-tuple-element.882) | copy-start | bytes 4718596
  72.5 22.6 %collective-permute-start = (bf16[2,2,128,768]{2,3,1,0:T(8,128)(2,1)}, bf16[2,2,128,768]{2,3,1,0:T(8,128)(2,1)S(1)}, u32[]{:S(2)}, u32[]{:S(2)}) collective-permute-start(bf16[2,2,128,768]{2,3,1,0:T(8,128)(2,1)} %get-tuple-element.1078), channel_id=1, source_target_pairs={{28,0},{0,4},{4,8},{8,12},{12,16},{16,20},{20,24},{24,28},{29,1},{... | collective-permute-start | bytes 2359304 | tf_op jit(solution)/shard_map/while/body/eval_jaxpr/ppermute | solution.py:20
  97.4 21.8 %collective-permute-start = (bf16[2,2,128,768]{2,3,1,0:T(8,128)(2,1)}, bf16[2,2,128,768]{2,3,1,0:T(8,128)(2,1)S(1)}, u32[]{:S(2)}, u32[]{:S(2)}) collective-permute-start(bf16[2,2,128,768]{2,3,1,0:T(8,128)(2,1)} %get-tuple-element.1078), channel_id=1, source_target_pairs={{28,0},{0,4},{4,8},{8,12},{12,16},{16,20},{20,24},{24,28},{29,1},{... | collective-permute-start | bytes 2359304 | tf_op jit(solution)/shard_map/while/body/eval_jaxpr/ppermute | solution.py:20
  121.4 20.8 %collective-permute-start = (bf16[2,2,128,768]{2,3,1,0:T(8,128)(2,1)}, bf16[2,2,128,768]{2,3,1,0:T(8,128)(2,1)S(1)}, u32[]{:S(2)}, u32[]{:S(2)}) collective-permute-start(bf16[2,2,128,768]{2,3,1,0:T(8,128)(2,1)} %get-tuple-element.1078), channel_id=1, source_target_pairs={{28,0},{0,4},{4,8},{8,12},{12,16},{16,20},{20,24},{24,28},{29,1},{... | collective-permute-start | bytes 2359304 | tf_op jit(solution)/shard_map/while/body/eval_jaxpr/ppermute | solution.py:20
  144.5 19.9 %collective-permute-start = (bf16[2,2,128,768]{2,3,1,0:T(8,128)(2,1)}, bf16[2,2,128,768]{2,3,1,0:T(8,128)(2,1)S(1)}, u32[]{:S(2)}, u32[]{:S(2)}) collective-permute-start(bf16[2,2,128,768]{2,3,1,0:T(8,128)(2,1)} %get-tuple-element.1078), channel_id=1, source_target_pairs={{28,0},{0,4},{4,8},{8,12},{12,16},{16,20},{20,24},{24,28},{29,1},{... | collective-permute-start | bytes 2359304 | tf_op jit(solution)/shard_map/while/body/eval_jaxpr/ppermute | solution.py:20
  166.7 19.0 %collective-permute-start = (bf16[2,2,128,768]{2,3,1,0:T(8,128)(2,1)}, bf16[2,2,128,768]{2,3,1,0:T(8,128)(2,1)S(1)}, u32[]{:S(2)}, u32[]{:S(2)}) collective-permute-start(bf16[2,2,128,768]{2,3,1,0:T(8,128)(2,1)} %get-tuple-element.1078), channel_id=1, source_target_pairs={{28,0},{0,4},{4,8},{8,12},{12,16},{16,20},{20,24},{24,28},{29,1},{... | collective-permute-start | bytes 2359304 | tf_op jit(solution)/shard_map/while/body/eval_jaxpr/ppermute | solution.py:20
  188.0 18.1 %collective-permute-start = (bf16[2,2,128,768]{2,3,1,0:T(8,128)(2,1)}, bf16[2,2,128,768]{2,3,1,0:T(8,128)(2,1)S(1)}, u32[]{:S(2)}, u32[]{:S(2)}) collective-permute-start(bf16[2,2,128,768]{2,3,1,0:T(8,128)(2,1)} %get-tuple-element.1078), channel_id=1, source_target_pairs={{28,0},{0,4},{4,8},{8,12},{12,16},{16,20},{20,24},{24,28},{29,1},{... | collective-permute-start | bytes 2359304 | tf_op jit(solution)/shard_map/while/body/eval_jaxpr/ppermute | solution.py:20
  208.3 17.2 %collective-permute-start = (bf16[2,2,128,768]{2,3,1,0:T(8,128)(2,1)}, bf16[2,2,128,768]{2,3,1,0:T(8,128)(2,1)S(1)}, u32[]{:S(2)}, u32[]{:S(2)}) collective-permute-start(bf16[2,2,128,768]{2,3,1,0:T(8,128)(2,1)} %get-tuple-element.1078), channel_id=1, source_target_pairs={{28,0},{0,4},{4,8},{8,12},{12,16},{16,20},{20,24},{24,28},{29,1},{... | collective-permute-start | bytes 2359304 | tf_op jit(solution)/shard_map/while/body/eval_jaxpr/ppermute | solution.py:20
  232.3 64.9 %copy-start.14 = (f32[256,768]{1,0:T(8,128)}, f32[256,768]{1,0:T(8,128)S(1)}, u32[]{:S(2)}) copy-start(f32[256,768]{1,0:T(8,128)S(1)} %get-tuple-element.884) | copy-start | bytes 2359300
  249.3 45.7 %copy-start.23 = (f32[256,768]{1,0:T(8,128)}, f32[256,768]{1,0:T(8,128)S(1)}, u32[]{:S(2)}) copy-start(f32[256,768]{1,0:T(8,128)S(1)} %get-tuple-element.887) | copy-start | bytes 2359300
  307.9 21.6 %collective-permute-start.3 = (bf16[2,2,128,768]{2,3,1,0:T(8,128)(2,1)}, bf16[2,2,128,768]{2,3,1,0:T(8,128)(2,1)S(1)}, u32[]{:S(2)}, u32[]{:S(2)}) collective-permute-start(bf16[2,2,128,768]{2,3,1,0:T(8,128)(2,1)} %pad_maximum_fusion.1), channel_id=1, source_target_pairs={{28,0},{0,4},{4,8},{8,12},{12,16},{16,20},{20,24},{24,28},{29,1},{... | collective-permute-start | bytes 2359304 | tf_op jit(solution)/shard_map/ppermute | solution.py:20
  311.8 331.9 %reduce-scatter.9.cloned.1.call-start = ((), (), s32[]{:S(2)}) async-start(), calls=%async_computation.13 | async-start | bytes 1474560 | tf_op jit(solution)/shard_map/reduce_scatter | solution.py:348
  329.7 20.7 %collective-permute-start.1 = (bf16[2,2,128,768]{2,3,1,0:T(8,128)(2,1)}, bf16[2,2,128,768]{2,3,1,0:T(8,128)(2,1)S(1)}, u32[]{:S(2)}, u32[]{:S(2)}) collective-permute-start(bf16[2,2,128,768]{2,3,1,0:T(8,128)(2,1)} %get-tuple-element.1127), channel_id=1, source_target_pairs={{28,0},{0,4},{4,8},{8,12},{12,16},{16,20},{20,24},{24,28},{29,1},{... | collective-permute-start | bytes 2359304 | tf_op jit(solution)/shard_map/while/body/eval_jaxpr/ppermute | solution.py:20
  352.9 19.6 %collective-permute-start.2 = (bf16[2,2,128,768]{2,3,1,0:T(8,128)(2,1)S(1)}, bf16[2,2,128,768]{2,3,1,0:T(8,128)(2,1)S(1)}, u32[]{:S(2)}, u32[]{:S(2)}) collective-permute-start(bf16[2,2,128,768]{2,3,1,0:T(8,128)(2,1)S(1)} %fusion.222), channel_id=1, source_target_pairs={{28,0},{0,4},{4,8},{8,12},{12,16},{16,20},{20,24},{24,28},{29,1},{... | collective-permute-start | bytes 2359304 | tf_op jit(solution)/shard_map/while/body/eval_jaxpr/ppermute | solution.py:20
  354.7 17.7 %copy-start.57 = (f32[12,32]{1,0:T(8,128)}, f32[12,32]{1,0:T(8,128)S(1)}, u32[]{:S(2)}) copy-start(f32[12,32]{1,0:T(8,128)S(1)} %fusion.224) | copy-start | bytes 4612 | tf_op jit(solution)/shard_map/while
  372.4 18.8 %collective-permute-start.1 = (bf16[2,2,128,768]{2,3,1,0:T(8,128)(2,1)}, bf16[2,2,128,768]{2,3,1,0:T(8,128)(2,1)S(1)}, u32[]{:S(2)}, u32[]{:S(2)}) collective-permute-start(bf16[2,2,128,768]{2,3,1,0:T(8,128)(2,1)} %get-tuple-element.1127), channel_id=1, source_target_pairs={{28,0},{0,4},{4,8},{8,12},{12,16},{16,20},{20,24},{24,28},{29,1},{... | collective-permute-start | bytes 2359304 | tf_op jit(solution)/shard_map/while/body/eval_jaxpr/ppermute | solution.py:20
  393.7 17.7 %collective-permute-start.2 = (bf16[2,2,128,768]{2,3,1,0:T(8,128)(2,1)S(1)}, bf16[2,2,128,768]{2,3,1,0:T(8,128)(2,1)S(1)}, u32[]{:S(2)}, u32[]{:S(2)}) collective-permute-start(bf16[2,2,128,768]{2,3,1,0:T(8,128)(2,1)S(1)} %fusion.222), channel_id=1, source_target_pairs={{28,0},{0,4},{4,8},{8,12},{12,16},{16,20},{20,24},{24,28},{29,1},{... | collective-permute-start | bytes 2359304 | tf_op jit(solution)/shard_map/while/body/eval_jaxpr/ppermute | solution.py:20
  395.6 15.8 %copy-start.57 = (f32[12,32]{1,0:T(8,128)}, f32[12,32]{1,0:T(8,128)S(1)}, u32[]{:S(2)}) copy-start(f32[12,32]{1,0:T(8,128)S(1)} %fusion.224) | copy-start | bytes 4612 | tf_op jit(solution)/shard_map/while
  411.4 16.9 %collective-permute-start.1 = (bf16[2,2,128,768]{2,3,1,0:T(8,128)(2,1)}, bf16[2,2,128,768]{2,3,1,0:T(8,128)(2,1)S(1)}, u32[]{:S(2)}, u32[]{:S(2)}) collective-permute-start(bf16[2,2,128,768]{2,3,1,0:T(8,128)(2,1)} %get-tuple-element.1127), channel_id=1, source_target_pairs={{28,0},{0,4},{4,8},{8,12},{12,16},{16,20},{20,24},{24,28},{29,1},{... | collective-permute-start | bytes 2359304 | tf_op jit(solution)/shard_map/while/body/eval_jaxpr/ppermute | solution.py:20
  430.8 17.5 %collective-permute-start.2 = (bf16[2,2,128,768]{2,3,1,0:T(8,128)(2,1)S(1)}, bf16[2,2,128,768]{2,3,1,0:T(8,128)(2,1)S(1)}, u32[]{:S(2)}, u32[]{:S(2)}) collective-permute-start(bf16[2,2,128,768]{2,3,1,0:T(8,128)(2,1)S(1)} %fusion.222), channel_id=1, source_target_pairs={{28,0},{0,4},{4,8},{8,12},{12,16},{16,20},{20,24},{24,28},{29,1},{... | collective-permute-start | bytes 2359304 | tf_op jit(solution)/shard_map/while/body/eval_jaxpr/ppermute | solution.py:20
  432.7 15.7 %copy-start.57 = (f32[12,32]{1,0:T(8,128)}, f32[12,32]{1,0:T(8,128)S(1)}, u32[]{:S(2)}) copy-start(f32[12,32]{1,0:T(8,128)S(1)} %fusion.224) | copy-start | bytes 4612 | tf_op jit(solution)/shard_map/while
  448.4 15.4 %collective-permute-start.1 = (bf16[2,2,128,768]{2,3,1,0:T(8,128)(2,1)}, bf16[2,2,128,768]{2,3,1,0:T(8,128)(2,1)S(1)}, u32[]{:S(2)}, u32[]{:S(2)}) collective-permute-start(bf16[2,2,128,768]{2,3,1,0:T(8,128)(2,1)} %get-tuple-element.1127), channel_id=1, source_target_pairs={{28,0},{0,4},{4,8},{8,12},{12,16},{16,20},{20,24},{24,28},{29,1},{... | collective-permute-start | bytes 2359304 | tf_op jit(solution)/shard_map/while/body/eval_jaxpr/ppermute | solution.py:20
  466.3 18.4 %collective-permute-start.2 = (bf16[2,2,128,768]{2,3,1,0:T(8,128)(2,1)S(1)}, bf16[2,2,128,768]{2,3,1,0:T(8,128)(2,1)S(1)}, u32[]{:S(2)}, u32[]{:S(2)}) collective-permute-start(bf16[2,2,128,768]{2,3,1,0:T(8,128)(2,1)S(1)} %fusion.222), channel_id=1, source_target_pairs={{28,0},{0,4},{4,8},{8,12},{12,16},{16,20},{20,24},{24,28},{29,1},{... | collective-permute-start | bytes 2359304 | tf_op jit(solution)/shard_map/while/body/eval_jaxpr/ppermute | solution.py:20
  468.1 16.5 %copy-start.57 = (f32[12,32]{1,0:T(8,128)}, f32[12,32]{1,0:T(8,128)S(1)}, u32[]{:S(2)}) copy-start(f32[12,32]{1,0:T(8,128)S(1)} %fusion.224) | copy-start | bytes 4612 | tf_op jit(solution)/shard_map/while
  484.6 17.3 %collective-permute-start.1 = (bf16[2,2,128,768]{2,3,1,0:T(8,128)(2,1)}, bf16[2,2,128,768]{2,3,1,0:T(8,128)(2,1)S(1)}, u32[]{:S(2)}, u32[]{:S(2)}) collective-permute-start(bf16[2,2,128,768]{2,3,1,0:T(8,128)(2,1)} %get-tuple-element.1127), channel_id=1, source_target_pairs={{28,0},{0,4},{4,8},{8,12},{12,16},{16,20},{20,24},{24,28},{29,1},{... | collective-permute-start | bytes 2359304 | tf_op jit(solution)/shard_map/while/body/eval_jaxpr/ppermute | solution.py:20
  504.4 20.5 %collective-permute-start.2 = (bf16[2,2,128,768]{2,3,1,0:T(8,128)(2,1)S(1)}, bf16[2,2,128,768]{2,3,1,0:T(8,128)(2,1)S(1)}, u32[]{:S(2)}, u32[]{:S(2)}) collective-permute-start(bf16[2,2,128,768]{2,3,1,0:T(8,128)(2,1)S(1)} %fusion.222), channel_id=1, source_target_pairs={{28,0},{0,4},{4,8},{8,12},{12,16},{16,20},{20,24},{24,28},{29,1},{... | collective-permute-start | bytes 2359304 | tf_op jit(solution)/shard_map/while/body/eval_jaxpr/ppermute | solution.py:20
  506.2 18.6 %copy-start.57 = (f32[12,32]{1,0:T(8,128)}, f32[12,32]{1,0:T(8,128)S(1)}, u32[]{:S(2)}) copy-start(f32[12,32]{1,0:T(8,128)S(1)} %fusion.224) | copy-start | bytes 4612 | tf_op jit(solution)/shard_map/while
  524.9 19.4 %collective-permute-start.1 = (bf16[2,2,128,768]{2,3,1,0:T(8,128)(2,1)}, bf16[2,2,128,768]{2,3,1,0:T(8,128)(2,1)S(1)}, u32[]{:S(2)}, u32[]{:S(2)}) collective-permute-start(bf16[2,2,128,768]{2,3,1,0:T(8,128)(2,1)} %get-tuple-element.1127), channel_id=1, source_target_pairs={{28,0},{0,4},{4,8},{8,12},{12,16},{16,20},{20,24},{24,28},{29,1},{... | collective-permute-start | bytes 2359304 | tf_op jit(solution)/shard_map/while/body/eval_jaxpr/ppermute | solution.py:20
  546.8 22.8 %collective-permute-start.2 = (bf16[2,2,128,768]{2,3,1,0:T(8,128)(2,1)S(1)}, bf16[2,2,128,768]{2,3,1,0:T(8,128)(2,1)S(1)}, u32[]{:S(2)}, u32[]{:S(2)}) collective-permute-start(bf16[2,2,128,768]{2,3,1,0:T(8,128)(2,1)S(1)} %fusion.222), channel_id=1, source_target_pairs={{28,0},{0,4},{4,8},{8,12},{12,16},{16,20},{20,24},{24,28},{29,1},{... | collective-permute-start | bytes 2359304 | tf_op jit(solution)/shard_map/while/body/eval_jaxpr/ppermute | solution.py:20
  548.7 20.9 %copy-start.57 = (f32[12,32]{1,0:T(8,128)}, f32[12,32]{1,0:T(8,128)S(1)}, u32[]{:S(2)}) copy-start(f32[12,32]{1,0:T(8,128)S(1)} %fusion.224) | copy-start | bytes 4612 | tf_op jit(solution)/shard_map/while
  569.6 21.8 %collective-permute-start.1 = (bf16[2,2,128,768]{2,3,1,0:T(8,128)(2,1)}, bf16[2,2,128,768]{2,3,1,0:T(8,128)(2,1)S(1)}, u32[]{:S(2)}, u32[]{:S(2)}) collective-permute-start(bf16[2,2,128,768]{2,3,1,0:T(8,128)(2,1)} %get-tuple-element.1127), channel_id=1, source_target_pairs={{28,0},{0,4},{4,8},{8,12},{12,16},{16,20},{20,24},{24,28},{29,1},{... | collective-permute-start | bytes 2359304 | tf_op jit(solution)/shard_map/while/body/eval_jaxpr/ppermute | solution.py:20
  593.9 14.7 %collective-permute-start.2 = (bf16[2,2,128,768]{2,3,1,0:T(8,128)(2,1)S(1)}, bf16[2,2,128,768]{2,3,1,0:T(8,128)(2,1)S(1)}, u32[]{:S(2)}, u32[]{:S(2)}) collective-permute-start(bf16[2,2,128,768]{2,3,1,0:T(8,128)(2,1)S(1)} %fusion.222), channel_id=1, source_target_pairs={{28,0},{0,4},{4,8},{8,12},{12,16},{16,20},{20,24},{24,28},{29,1},{... | collective-permute-start | bytes 2359304 | tf_op jit(solution)/shard_map/while/body/eval_jaxpr/ppermute | solution.py:20
  595.7 12.9 %copy-start.57 = (f32[12,32]{1,0:T(8,128)}, f32[12,32]{1,0:T(8,128)S(1)}, u32[]{:S(2)}) copy-start(f32[12,32]{1,0:T(8,128)S(1)} %fusion.224) | copy-start | bytes 4612 | tf_op jit(solution)/shard_map/while
  611.2 53.4 %reduce-scatter.11.cloned.1.call-start = ((), (), s32[]{:S(2)}) async-start(), calls=%async_computation.14 | async-start | bytes 1474560 | tf_op jit(solution)/shard_map/reduce_scatter | solution.py:351
  612.9 80.7 %reduce-scatter.7.cloned.1.call-start = ((), (), s32[]{:S(2)}) async-start(), calls=%async_computation.12 | async-start | bytes 1474560 | tf_op jit(solution)/shard_map/reduce_scatter | solution.py:345
  615.0 129.0 %reduce-scatter.15.cloned.1.call-start = ((), (), s32[]{:S(2)}) async-start(), calls=%async_computation.16 | async-start | bytes 5898240 | tf_op jit(solution)/shard_map/reduce_scatter | solution.py:363
  620.3 174.1 %reduce-scatter.17.cloned.1.call-start = ((), (), s32[]{:S(2)}) async-start(), calls=%async_computation.17 | async-start | bytes 5898240 | tf_op jit(solution)/shard_map/reduce_scatter | solution.py:366
  630.5 12.0 %copy-start.3 = (f32[256,768]{1,0:T(8,128)S(1)}, f32[256,768]{1,0:T(8,128)}, u32[]{:S(2)}) copy-start(f32[256,768]{1,0:T(8,128)} %copy-done.2) | copy-start | bytes 2359300
  (105 other events, 276.6 us)
Sparse Core Ops, SparseCore 0:
  9.6 20.2 all-gather.10
  31.5 17.5 all-gather.6
  50.6 17.4 all-gather.8
  69.5 17.4 all-gather.12
  88.4 37.4 all-gather.14
  127.3 37.4 all-gather.16
  311.9 25.7 reduce-scatter.12
  611.4 24.8 reduce-scatter.8
  638.8 25.8 reduce-scatter.10
  667.8 25.7 reduce-scatter.6
  696.1 47.8 reduce-scatter.14
  746.5 47.7 reduce-scatter.16
where the time goes:
time: 1090 us; the launch traced here: 1080 us
  waiting for transfers between devices  554 us (51%)
  blocking collectives  341 us (31%)
  matrix products  97.1 us (9%)
  local copies, waits for them, and re-layouts  35.9 us (3%)
  other arithmetic  25.6 us (2%)
  between operations  20.7 us (2%)
    ppermute x22, waiting for transfers between devices, passed_along(): return lax.ppermute(block, axis, route)  371 us
    psum x1, blocking collectives, on_device(): lax.psum((shares[0], shares[1], shares[2], shares[3], shares[4], shares[5...  279 us
    reduce_scatter x1, waiting for transfers between devices, on_device(): lax.psum_scatter(local_grads[8].astype(jnp.bfloat16), 'wsh', scatter_dime...  50.4 us
    reduce_scatter x1, waiting for transfers between devices, on_device(): lax.psum_scatter(local_grads[7].astype(jnp.bfloat16), 'wsh', scatter_dime...  50.4 us
    psum x1, blocking collectives, on_device(): lax.psum((jnp.sum(deviation * deviation * row_valid), jnp.sum(row_valid))...  37.3 us
    reduce_scatter x1, waiting for transfers between devices, on_device(): lax.psum_scatter(local_grads[1].astype(jnp.bfloat16), 'wsh', scatter_dime...  28.9 us
  transfers between devices with their start and end apart: 34, of which 28 were waited for; matrix products, arithmetic and copies ran while one was open for 12% of the time, Pallas kernels for 0%

commit v1 on v0

--- a/solution.py
+++ b/solution.py
@@ -222,7 +222,7 @@
     )
     deviation = result - teacher.reshape(row_count, D).astype(jnp.float32)
     square_sum, valid_count = lax.psum(
-        (jnp.sum(deviation * deviation * row_valid), jnp.sum(row_valid)), ("ctx", "wsh")
+        lax.psum((jnp.sum(deviation * deviation * row_valid), jnp.sum(row_valid)), "ctx"), "wsh"
     )
     loss_value = square_sum / (valid_count * D)
     result_grad = token_total / valid_count * deviation * row_valid

time: 1090 us -> 1060 us (0.972)
  waiting for transfers between devices: 554 us -> 533 us
    psum x1 -> x2, blocking collectives: 279 us -> 13.5 us  [on_device(): lax.psum(lax.psum((jnp.sum(deviation * deviation * row_valid), jnp.sum(ro...]
    psum x1 -> x2, blocking collectives: 37.3 us -> 301 us  [on_device(): lax.psum((jnp.sum(deviation * deviation * row_valid), jnp.sum(row_valid))...]
    all_gather x1, waiting for transfers between devices: 14 us -> 0.01 us  [on_device(): lax.all_gather(shards[3], 'wsh', axis=0, tiled=True)]
    all_gather x1, waiting for transfers between devices: 14 us -> 0.02 us  [on_device(): lax.all_gather(shards[2], 'wsh', axis=0, tiled=True)]
  transfers between devices with their start and end apart: 34 -> 34, of which waited for: 28 -> 26; matrix products, arithmetic and copies ran while one was open for 12% -> 12% of each run, Pallas kernels for 0% -> 0%
where the time goes in v1:
time: 1060 us; the launch traced here: 1050 us
  waiting for transfers between devices  533 us (50%)
  blocking collectives  339 us (32%)
  matrix products  96.1 us (9%)
  local copies, waits for them, and re-layouts  35.7 us (3%)
  other arithmetic  24.3 us (2%)
  between operations  20.7 us (2%)
    ppermute x22, waiting for transfers between devices, passed_along(): return lax.ppermute(block, axis, route)  377 us
    psum x2, blocking collectives, on_device(): lax.psum((jnp.sum(deviation * deviation * row_valid), jnp.sum(row_valid))...  301 us
    reduce_scatter x1, waiting for transfers between devices, on_device(): lax.psum_scatter(local_grads[7].astype(jnp.bfloat16), 'wsh', scatter_dime...  50.4 us
    reduce_scatter x1, waiting for transfers between devices, on_device(): lax.psum_scatter(local_grads[8].astype(jnp.bfloat16), 'wsh', scatter_dime...  50.4 us
    reduce_scatter x1, waiting for transfers between devices, on_device(): lax.psum_scatter(local_grads[1].astype(jnp.bfloat16), 'wsh', scatter_dime...  28.9 us
    reduce_scatter x1, waiting for transfers between devices, on_device(): lax.psum_scatter(local_grads[3].astype(jnp.bfloat16), 'wsh', scatter_dime...  22.5 us
  transfers between devices with their start and end apart: 34, of which 26 were waited for; matrix products, arithmetic and copies ran while one was open for 12% of the time, Pallas kernels for 0%

profile of v1, /device:TPU:0, one launch (start us, length us, event | category | flops | bytes accessed | tf_op | source)
XLA Modules:
  0.0 1051.9 jit_solution(11832547324350513851)
XLA Ops:
  13.8 8.3 all-reduce.7
  22.3 5.2 all_gather.31
  30.8 22.3 %psum.93 = f32[]{:T(128)} all-reduce(f32[]{:T(128)} %get-tuple-element.854), channel_id=1, replica_groups=mesh['ctx'=8,'wsh'=4] {'ctx'}, use_global_device_ids=true, to_apply=%region_12.13 | all-reduce | flops 1 | bytes 8 | tf_op jit(solution)/shard_map/psum | solution.py:225
  53.6 7.0 psum.94
  63.0 1.8 convolution_convert_fusion.9
  65.1 1.9 convolution_convert_fusion.11
  70.2 1.7 convolution_convert_fusion.10
  74.1 151.0 %while.44 = (s32[]{:T(128)}, bf16[2,2,128,768]{2,3,1,0:T(8,128)(2,1)}, f32[2,12,128]{2,1,0:T(8,128)S(1)}, f32[2,12,128]{2,1,0:T(8,128)}, f32[2,128,12,64]{1,3,2,...) while((s32[]{:T(128)}, ...), condition=%wide.region_6.7_spmd.clone, body=%wide.region_3.6_spmd.clone.sunk | while | flops 117384720 | bytes 21013696 | solution.py:201
  76.1 20.1 %collective-permute-done = bf16[2,2,128,768]{2,3,1,0:T(8,128)(2,1)S(1)} collective-permute-done((bf16[2,2,128,768]{2,3,1,0:T(8,128)(2,1)}, bf16[2,2,128,768]{2,3,1,0:T(8,128)(2,1)S(1)}, u32[]{:S(2)}, u32[]{:S(2)}) %collective-permute-start) | collective-permute-done | bytes 786464 | tf_op jit(solution)/shard_map/while/body/eval_jaxpr/ppermute | solution.py:20
  100.4 19.2 %collective-permute-done = bf16[2,2,128,768]{2,3,1,0:T(8,128)(2,1)S(1)} collective-permute-done((bf16[2,2,128,768]{2,3,1,0:T(8,128)(2,1)}, bf16[2,2,128,768]{2,3,1,0:T(8,128)(2,1)S(1)}, u32[]{:S(2)}, u32[]{:S(2)}) %collective-permute-start) | collective-permute-done | bytes 786464 | tf_op jit(solution)/shard_map/while/body/eval_jaxpr/ppermute | solution.py:20
  123.8 18.3 %collective-permute-done = bf16[2,2,128,768]{2,3,1,0:T(8,128)(2,1)S(1)} collective-permute-done((bf16[2,2,128,768]{2,3,1,0:T(8,128)(2,1)}, bf16[2,2,128,768]{2,3,1,0:T(8,128)(2,1)S(1)}, u32[]{:S(2)}, u32[]{:S(2)}) %collective-permute-start) | collective-permute-done | bytes 786464 | tf_op jit(solution)/shard_map/while/body/eval_jaxpr/ppermute | solution.py:20
  146.3 17.4 %collective-permute-done = bf16[2,2,128,768]{2,3,1,0:T(8,128)(2,1)S(1)} collective-permute-done((bf16[2,2,128,768]{2,3,1,0:T(8,128)(2,1)}, bf16[2,2,128,768]{2,3,1,0:T(8,128)(2,1)S(1)}, u32[]{:S(2)}, u32[]{:S(2)}) %collective-permute-start) | collective-permute-done | bytes 786464 | tf_op jit(solution)/shard_map/while/body/eval_jaxpr/ppermute | solution.py:20
  167.9 16.5 %collective-permute-done = bf16[2,2,128,768]{2,3,1,0:T(8,128)(2,1)S(1)} collective-permute-done((bf16[2,2,128,768]{2,3,1,0:T(8,128)(2,1)}, bf16[2,2,128,768]{2,3,1,0:T(8,128)(2,1)S(1)}, u32[]{:S(2)}, u32[]{:S(2)}) %collective-permute-start) | collective-permute-done | bytes 786464 | tf_op jit(solution)/shard_map/while/body/eval_jaxpr/ppermute | solution.py:20
  188.5 15.5 %collective-permute-done = bf16[2,2,128,768]{2,3,1,0:T(8,128)(2,1)S(1)} collective-permute-done((bf16[2,2,128,768]{2,3,1,0:T(8,128)(2,1)}, bf16[2,2,128,768]{2,3,1,0:T(8,128)(2,1)S(1)}, u32[]{:S(2)}, u32[]{:S(2)}) %collective-permute-start) | collective-permute-done | bytes 786464 | tf_op jit(solution)/shard_map/while/body/eval_jaxpr/ppermute | solution.py:20
  208.3 14.6 %collective-permute-done = bf16[2,2,128,768]{2,3,1,0:T(8,128)(2,1)S(1)} collective-permute-done((bf16[2,2,128,768]{2,3,1,0:T(8,128)(2,1)}, bf16[2,2,128,768]{2,3,1,0:T(8,128)(2,1)S(1)}, u32[]{:S(2)}, u32[]{:S(2)}) %collective-permute-start) | collective-permute-done | bytes 786464 | tf_op jit(solution)/shard_map/while/body/eval_jaxpr/ppermute | solution.py:20
  227.6 2.1 multiply_reduce_fusion.4
  230.4 11.3 %multiply_convert_fusion.1 = (bf16[256,3072]{1,0:T(8,128)(2,1)S(1)}, f32[256,3072]{1,0:T(8,128)}, f32[256,3072]{1,0:T(8,128)}) fusion(bf16[768,3072]{1,0:T(8,128)(2,1)} %all-gather.15.cloned.1.call-done, f32[256,768]{1,0:T(8,128)S(1)} %get-tuple-element.884, f32[768]{0:T(1024)S(1)} %copy-done.42, f32[256]{0:T(256)S(1)} %fusion.98), kind=kOutput, calls=%fused_computation.67 | convolution fusion | flops 1259667456 | bytes 13373440 | tf_op jit(solution)/shard_map/dot_general | solution.py:216
  241.8 4.3 fusion.71
  246.2 5.2 add_convert_fusion
  251.5 2.1 multiply_reduce_fusion
  253.6 2.6 fusion.57
  265.8 2.6 convolution_convert_fusion.2
  268.4 2.1 fusion.49
  270.9 10.9 %collective-permute-done.3 = bf16[2,2,128,768]{2,3,1,0:T(8,128)(2,1)S(1)} collective-permute-done((bf16[2,2,128,768]{2,3,1,0:T(8,128)(2,1)}, bf16[2,2,128,768]{2,3,1,0:T(8,128)(2,1)S(1)}, u32[]{:S(2)}, u32[]{:S(2)}) %collective-permute-start.3) | collective-permute-done | bytes 786464 | tf_op jit(solution)/shard_map/ppermute | solution.py:20
  281.8 291.3 %while.45 = (s32[]{:T(128)}, bf16[2,2,128,768]{2,3,1,0:T(8,128)(2,1)}, bf16[2,2,128,768]{2,3,1,0:T(8,128)(2,1)S(1)}, f32[2,128,12,64]{1,3,2,0:T(8,128)S(1)}, f32...) while((s32[]{:T(128)}, ...), condition=%wide.region_19.20_spmd.clone, body=%wide.region_17.19_spmd.clone.sunk | while | flops 283444096 | bytes 33844516 | solution.py:308
  283.7 14.1 %collective-permute-done.1 = bf16[2,2,128,768]{2,3,1,0:T(8,128)(2,1)S(1)} collective-permute-done((bf16[2,2,128,768]{2,3,1,0:T(8,128)(2,1)}, bf16[2,2,128,768]{2,3,1,0:T(8,128)(2,1)S(1)}, u32[]{:S(2)}, u32[]{:S(2)}) %collective-permute-start.1) | collective-permute-done | bytes 786464 | tf_op jit(solution)/shard_map/while/body/eval_jaxpr/ppermute | solution.py:20
  302.8 16.5 %collective-permute-done.2 = bf16[2,2,128,768]{2,3,1,0:T(8,128)(2,1)S(1)} collective-permute-done((bf16[2,2,128,768]{2,3,1,0:T(8,128)(2,1)S(1)}, bf16[2,2,128,768]{2,3,1,0:T(8,128)(2,1)S(1)}, u32[]{:S(2)}, u32[]{:S(2)}) %collective-permute-start.2) | collective-permute-done | bytes 786464 | tf_op jit(solution)/shard_map/while/body/eval_jaxpr/ppermute | solution.py:20
  320.9 16.3 %collective-permute-done.1 = bf16[2,2,128,768]{2,3,1,0:T(8,128)(2,1)S(1)} collective-permute-done((bf16[2,2,128,768]{2,3,1,0:T(8,128)(2,1)}, bf16[2,2,128,768]{2,3,1,0:T(8,128)(2,1)S(1)}, u32[]{:S(2)}, u32[]{:S(2)}) %collective-permute-start.1) | collective-permute-done | bytes 786464 | tf_op jit(solution)/shard_map/while/body/eval_jaxpr/ppermute | solution.py:20
  342.2 18.6 %collective-permute-done.2 = bf16[2,2,128,768]{2,3,1,0:T(8,128)(2,1)S(1)} collective-permute-done((bf16[2,2,128,768]{2,3,1,0:T(8,128)(2,1)S(1)}, bf16[2,2,128,768]{2,3,1,0:T(8,128)(2,1)S(1)}, u32[]{:S(2)}, u32[]{:S(2)}) %collective-permute-start.2) | collective-permute-done | bytes 786464 | tf_op jit(solution)/shard_map/while/body/eval_jaxpr/ppermute | solution.py:20
  362.4 18.4 %collective-permute-done.1 = bf16[2,2,128,768]{2,3,1,0:T(8,128)(2,1)S(1)} collective-permute-done((bf16[2,2,128,768]{2,3,1,0:T(8,128)(2,1)}, bf16[2,2,128,768]{2,3,1,0:T(8,128)(2,1)S(1)}, u32[]{:S(2)}, u32[]{:S(2)}) %collective-permute-start.1) | collective-permute-done | bytes 786464 | tf_op jit(solution)/shard_map/while/body/eval_jaxpr/ppermute | solution.py:20
  385.8 20.4 %collective-permute-done.2 = bf16[2,2,128,768]{2,3,1,0:T(8,128)(2,1)S(1)} collective-permute-done((bf16[2,2,128,768]{2,3,1,0:T(8,128)(2,1)S(1)}, bf16[2,2,128,768]{2,3,1,0:T(8,128)(2,1)S(1)}, u32[]{:S(2)}, u32[]{:S(2)}) %collective-permute-start.2) | collective-permute-done | bytes 786464 | tf_op jit(solution)/shard_map/while/body/eval_jaxpr/ppermute | solution.py:20
  407.9 20.4 %collective-permute-done.1 = bf16[2,2,128,768]{2,3,1,0:T(8,128)(2,1)S(1)} collective-permute-done((bf16[2,2,128,768]{2,3,1,0:T(8,128)(2,1)}, bf16[2,2,128,768]{2,3,1,0:T(8,128)(2,1)S(1)}, u32[]{:S(2)}, u32[]{:S(2)}) %collective-permute-start.1) | collective-permute-done | bytes 786464 | tf_op jit(solution)/shard_map/while/body/eval_jaxpr/ppermute | solution.py:20
  433.3 18.5 %collective-permute-done.2 = bf16[2,2,128,768]{2,3,1,0:T(8,128)(2,1)S(1)} collective-permute-done((bf16[2,2,128,768]{2,3,1,0:T(8,128)(2,1)S(1)}, bf16[2,2,128,768]{2,3,1,0:T(8,128)(2,1)S(1)}, u32[]{:S(2)}, u32[]{:S(2)}) %collective-permute-start.2) | collective-permute-done | bytes 786464 | tf_op jit(solution)/shard_map/while/body/eval_jaxpr/ppermute | solution.py:20
  453.4 20.9 %collective-permute-done.1 = bf16[2,2,128,768]{2,3,1,0:T(8,128)(2,1)S(1)} collective-permute-done((bf16[2,2,128,768]{2,3,1,0:T(8,128)(2,1)}, bf16[2,2,128,768]{2,3,1,0:T(8,128)(2,1)S(1)}, u32[]{:S(2)}, u32[]{:S(2)}) %collective-permute-start.1) | collective-permute-done | bytes 786464 | tf_op jit(solution)/shard_map/while/body/eval_jaxpr/ppermute | solution.py:20
  479.4 16.8 %collective-permute-done.2 = bf16[2,2,128,768]{2,3,1,0:T(8,128)(2,1)S(1)} collective-permute-done((bf16[2,2,128,768]{2,3,1,0:T(8,128)(2,1)S(1)}, bf16[2,2,128,768]{2,3,1,0:T(8,128)(2,1)S(1)}, u32[]{:S(2)}, u32[]{:S(2)}) %collective-permute-start.2) | collective-permute-done | bytes 786464 | tf_op jit(solution)/shard_map/while/body/eval_jaxpr/ppermute | solution.py:20
  497.8 19.2 %collective-permute-done.1 = bf16[2,2,128,768]{2,3,1,0:T(8,128)(2,1)S(1)} collective-permute-done((bf16[2,2,128,768]{2,3,1,0:T(8,128)(2,1)}, bf16[2,2,128,768]{2,3,1,0:T(8,128)(2,1)S(1)}, u32[]{:S(2)}, u32[]{:S(2)}) %collective-permute-start.1) | collective-permute-done | bytes 786464 | tf_op jit(solution)/shard_map/while/body/eval_jaxpr/ppermute | solution.py:20
  521.9 14.9 %collective-permute-done.2 = bf16[2,2,128,768]{2,3,1,0:T(8,128)(2,1)S(1)} collective-permute-done((bf16[2,2,128,768]{2,3,1,0:T(8,128)(2,1)S(1)}, bf16[2,2,128,768]{2,3,1,0:T(8,128)(2,1)S(1)}, u32[]{:S(2)}, u32[]{:S(2)}) %collective-permute-start.2) | collective-permute-done | bytes 786464 | tf_op jit(solution)/shard_map/while/body/eval_jaxpr/ppermute | solution.py:20
  538.5 17.3 %collective-permute-done.1 = bf16[2,2,128,768]{2,3,1,0:T(8,128)(2,1)S(1)} collective-permute-done((bf16[2,2,128,768]{2,3,1,0:T(8,128)(2,1)}, bf16[2,2,128,768]{2,3,1,0:T(8,128)(2,1)S(1)}, u32[]{:S(2)}, u32[]{:S(2)}) %collective-permute-start.1) | collective-permute-done | bytes 786464 | tf_op jit(solution)/shard_map/while/body/eval_jaxpr/ppermute | solution.py:20
  560.8 12.2 %collective-permute-done.2 = bf16[2,2,128,768]{2,3,1,0:T(8,128)(2,1)S(1)} collective-permute-done((bf16[2,2,128,768]{2,3,1,0:T(8,128)(2,1)S(1)}, bf16[2,2,128,768]{2,3,1,0:T(8,128)(2,1)S(1)}, u32[]{:S(2)}, u32[]{:S(2)}) %collective-permute-start.2) | collective-permute-done | bytes 786464 | tf_op jit(solution)/shard_map/while/body/eval_jaxpr/ppermute | solution.py:20
  579.5 3.6 convolution_convert_fusion
  584.8 3.7 convolution_convert_fusion.1
  593.6 10.3 all-reduce.6
  605.2 22.5 %reduce-scatter.11.cloned.1.call-done = bf16[192,768]{1,0:T(8,128)(2,1)} async-done(((bf16[768,768]{1,0:T(8,128)(2,1)}), bf16[192,768]{1,0:T(8,128)(2,1)}) %reduce-scatter.11.cloned.1.call-update) | async-done | bytes 294928 | tf_op jit(solution)/shard_map/reduce_scatter | solution.py:351
  627.7 28.9 %reduce-scatter.7.cloned.1.call-done = bf16[192,768]{1,0:T(8,128)(2,1)} async-done(((bf16[768,768]{1,0:T(8,128)(2,1)}), bf16[192,768]{1,0:T(8,128)(2,1)}) %reduce-scatter.7.cloned.1.call-update) | async-done | bytes 294928 | tf_op jit(solution)/shard_map/reduce_scatter | solution.py:345
  656.6 50.4 %reduce-scatter.17.cloned.1.call-done = bf16[768,768]{1,0:T(8,128)(2,1)} async-done(((bf16[3072,768]{1,0:T(8,128)(2,1)}), bf16[768,768]{1,0:T(8,128)(2,1)}) %reduce-scatter.17.cloned.1.call-update) | async-done | bytes 1179664 | tf_op jit(solution)/shard_map/reduce_scatter | solution.py:366
  707.0 50.4 %reduce-scatter.15.cloned.1.call-done = bf16[192,3072]{1,0:T(8,128)(2,1)} async-done(((bf16[768,3072]{1,0:T(8,128)(2,1)}), bf16[192,3072]{1,0:T(8,128)(2,1)}) %reduce-scatter.15.cloned.1.call-update) | async-done | bytes 1179664 | tf_op jit(solution)/shard_map/reduce_scatter | solution.py:363
  757.4 279.0 %all-reduce.9 = (f32[]{:T(128)}, f32[192]{0:T(256)}, f32[192,768]{1,0:T(8,128)}, f32[192,768]{1,0:T(8,128)}, f32[192,768]{1,0:T(8,128)}, /*index=5*/f32[192,768]...) all-reduce(f32[]{:T(128)} %get-tuple-element.873, ...), channel_id=1, replica_groups=mesh['ctx'=8,'wsh'=4] {'ctx'}, use_global_device_ids=true, to_apply=%region_9.10 | all-reduce | flops 1769953 | bytes 10620680 | tf_op jit(solution)/shard_map/psum | solution.py:225
  1036.5 6.5 psum.92
  (585 shorter events, 116.0 us)
Async XLA Ops:
  7.2 15.1 %copy-start.58 = (bf16[8,12]{1,0:T(8,128)(2,1)S(1)}, bf16[8,12]{1,0:T(8,128)(2,1)}, u32[]{:S(2)}) copy-start(bf16[8,12]{1,0:T(8,128)(2,1)} %param.24) | copy-start | bytes 580
  7.2 55.8 %all-gather.11.cloned.1.call-start = ((), (), s32[]{:S(2)}) async-start(), calls=%async_computation.8 | async-start | bytes 1474560 | tf_op jit(solution)/shard_map/all_gather | solution.py:87
  8.0 57.1 %all-gather.7.cloned.1.call-start = ((), (), s32[]{:S(2)}) async-start(), calls=%async_computation.6 | async-start | bytes 1474560 | tf_op jit(solution)/shard_map/all_gather | solution.py:88
  8.7 61.5 %all-gather.9.cloned.1.call-start = ((), (), s32[]{:S(2)}) async-start(), calls=%async_computation.7 | async-start | bytes 1474560 | tf_op jit(solution)/shard_map/all_gather | solution.py:89
  9.5 218.1 %all-gather.13.cloned.1.call-start = ((), (), s32[]{:S(2)}) async-start(), calls=%async_computation.9 | async-start | bytes 1474560 | tf_op jit(solution)/shard_map/all_gather | solution.py:90
  10.0 220.4 %all-gather.15.cloned.1.call-start = ((), (), s32[]{:S(2)}) async-start(), calls=%async_computation.10 | async-start | bytes 5898240 | tf_op jit(solution)/shard_map/all_gather | solution.py:93
  10.6 231.1 %all-gather.17.cloned.1.call-start = ((), (), s32[]{:S(2)}) async-start(), calls=%async_computation.11 | async-start | bytes 5898240 | tf_op jit(solution)/shard_map/all_gather | solution.py:94
  11.2 594.0 %reduce-scatter.13.cloned.1.call-start = ((), (), s32[]{:S(2)}) async-start(), calls=%async_computation.15 | async-start | bytes 1474560 | tf_op jit(solution)/shard_map/reduce_scatter | solution.py:354
  12.0 49.2 %copy-start.49 = (f32[256]{0:T(256)}, f32[256]{0:T(256)S(1)}, u32[]{:S(2)}) copy-start(f32[256]{0:T(256)S(1)} %bitcast_rsqrt_fusion) | copy-start | bytes 3076
  22.1 39.2 %copy-start.45 = (f32[768]{0:T(1024)}, f32[768]{0:T(1024)S(1)}, u32[]{:S(2)}) copy-start(f32[768]{0:T(1024)S(1)} %convert_element_type.491) | copy-start | bytes 9220
  74.1 22.1 %collective-permute-start = (bf16[2,2,128,768]{2,3,1,0:T(8,128)(2,1)}, bf16[2,2,128,768]{2,3,1,0:T(8,128)(2,1)S(1)}, u32[]{:S(2)}, u32[]{:S(2)}) collective-permute-start(bf16[2,2,128,768]{2,3,1,0:T(8,128)(2,1)} %get-tuple-element.1078), channel_id=1, source_target_pairs={{28,0},{0,4},{4,8},{8,12},{12,16},{16,20},{20,24},{24,28},{29,1},{... | collective-permute-start | bytes 2359304 | tf_op jit(solution)/shard_map/while/body/eval_jaxpr/ppermute | solution.py:20
  98.5 21.2 %collective-permute-start = (bf16[2,2,128,768]{2,3,1,0:T(8,128)(2,1)}, bf16[2,2,128,768]{2,3,1,0:T(8,128)(2,1)S(1)}, u32[]{:S(2)}, u32[]{:S(2)}) collective-permute-start(bf16[2,2,128,768]{2,3,1,0:T(8,128)(2,1)} %get-tuple-element.1078), channel_id=1, source_target_pairs={{28,0},{0,4},{4,8},{8,12},{12,16},{16,20},{20,24},{24,28},{29,1},{... | collective-permute-start | bytes 2359304 | tf_op jit(solution)/shard_map/while/body/eval_jaxpr/ppermute | solution.py:20
  121.9 20.2 %collective-permute-start = (bf16[2,2,128,768]{2,3,1,0:T(8,128)(2,1)}, bf16[2,2,128,768]{2,3,1,0:T(8,128)(2,1)S(1)}, u32[]{:S(2)}, u32[]{:S(2)}) collective-permute-start(bf16[2,2,128,768]{2,3,1,0:T(8,128)(2,1)} %get-tuple-element.1078), channel_id=1, source_target_pairs={{28,0},{0,4},{4,8},{8,12},{12,16},{16,20},{20,24},{24,28},{29,1},{... | collective-permute-start | bytes 2359304 | tf_op jit(solution)/shard_map/while/body/eval_jaxpr/ppermute | solution.py:20
  144.4 19.3 %collective-permute-start = (bf16[2,2,128,768]{2,3,1,0:T(8,128)(2,1)}, bf16[2,2,128,768]{2,3,1,0:T(8,128)(2,1)S(1)}, u32[]{:S(2)}, u32[]{:S(2)}) collective-permute-start(bf16[2,2,128,768]{2,3,1,0:T(8,128)(2,1)} %get-tuple-element.1078), channel_id=1, source_target_pairs={{28,0},{0,4},{4,8},{8,12},{12,16},{16,20},{20,24},{24,28},{29,1},{... | collective-permute-start | bytes 2359304 | tf_op jit(solution)/shard_map/while/body/eval_jaxpr/ppermute | solution.py:20
  166.0 18.4 %collective-permute-start = (bf16[2,2,128,768]{2,3,1,0:T(8,128)(2,1)}, bf16[2,2,128,768]{2,3,1,0:T(8,128)(2,1)S(1)}, u32[]{:S(2)}, u32[]{:S(2)}) collective-permute-start(bf16[2,2,128,768]{2,3,1,0:T(8,128)(2,1)} %get-tuple-element.1078), channel_id=1, source_target_pairs={{28,0},{0,4},{4,8},{8,12},{12,16},{16,20},{20,24},{24,28},{29,1},{... | collective-permute-start | bytes 2359304 | tf_op jit(solution)/shard_map/while/body/eval_jaxpr/ppermute | solution.py:20
  186.6 17.5 %collective-permute-start = (bf16[2,2,128,768]{2,3,1,0:T(8,128)(2,1)}, bf16[2,2,128,768]{2,3,1,0:T(8,128)(2,1)S(1)}, u32[]{:S(2)}, u32[]{:S(2)}) collective-permute-start(bf16[2,2,128,768]{2,3,1,0:T(8,128)(2,1)} %get-tuple-element.1078), channel_id=1, source_target_pairs={{28,0},{0,4},{4,8},{8,12},{12,16},{16,20},{20,24},{24,28},{29,1},{... | collective-permute-start | bytes 2359304 | tf_op jit(solution)/shard_map/while/body/eval_jaxpr/ppermute | solution.py:20
  206.3 16.5 %collective-permute-start = (bf16[2,2,128,768]{2,3,1,0:T(8,128)(2,1)}, bf16[2,2,128,768]{2,3,1,0:T(8,128)(2,1)S(1)}, u32[]{:S(2)}, u32[]{:S(2)}) collective-permute-start(bf16[2,2,128,768]{2,3,1,0:T(8,128)(2,1)} %get-tuple-element.1078), channel_id=1, source_target_pairs={{28,0},{0,4},{4,8},{8,12},{12,16},{16,20},{20,24},{24,28},{29,1},{... | collective-permute-start | bytes 2359304 | tf_op jit(solution)/shard_map/while/body/eval_jaxpr/ppermute | solution.py:20
  229.7 23.9 %copy-start.14 = (f32[256,768]{1,0:T(8,128)}, f32[256,768]{1,0:T(8,128)S(1)}, u32[]{:S(2)}) copy-start(f32[256,768]{1,0:T(8,128)S(1)} %get-tuple-element.884) | copy-start | bytes 2359300
  229.7 21.7 %copy-start.53 = (f32[256]{0:T(256)}, f32[256]{0:T(256)S(1)}, u32[]{:S(2)}) copy-start(f32[256]{0:T(256)S(1)} %fusion.98) | copy-start | bytes 3076
  230.4 11.4 %copy-start.39 = (bf16[2,128,768]{2,1,0:T(8,128)(2,1)S(1)}, bf16[2,128,768]{2,1,0:T(8,128)(2,1)}, u32[]{:S(2)}) copy-start(bf16[2,128,768]{2,1,0:T(8,128)(2,1)} %param.17) | copy-start | bytes 1179652
  230.4 11.4 %copy-start.61 = (f32[256]{0:T(256)S(1)}, f32[256]{0:T(256)}, u32[]{:S(2)}) copy-start(f32[256]{0:T(256)} %convert_bitcast_fusion.1) | copy-start | bytes 3076
  264.3 17.5 %collective-permute-start.3 = (bf16[2,2,128,768]{2,3,1,0:T(8,128)(2,1)}, bf16[2,2,128,768]{2,3,1,0:T(8,128)(2,1)S(1)}, u32[]{:S(2)}, u32[]{:S(2)}) collective-permute-start(bf16[2,2,128,768]{2,3,1,0:T(8,128)(2,1)} %pad_maximum_fusion.1), channel_id=1, source_target_pairs={{28,0},{0,4},{4,8},{8,12},{12,16},{16,20},{20,24},{24,28},{29,1},{... | collective-permute-start | bytes 2359304 | tf_op jit(solution)/shard_map/ppermute | solution.py:20
  268.4 336.8 %reduce-scatter.9.cloned.1.call-start = ((), (), s32[]{:S(2)}) async-start(), calls=%async_computation.13 | async-start | bytes 1474560 | tf_op jit(solution)/shard_map/reduce_scatter | solution.py:348
  282.0 15.8 %collective-permute-start.1 = (bf16[2,2,128,768]{2,3,1,0:T(8,128)(2,1)}, bf16[2,2,128,768]{2,3,1,0:T(8,128)(2,1)S(1)}, u32[]{:S(2)}, u32[]{:S(2)}) collective-permute-start(bf16[2,2,128,768]{2,3,1,0:T(8,128)(2,1)} %get-tuple-element.1127), channel_id=1, source_target_pairs={{28,0},{0,4},{4,8},{8,12},{12,16},{16,20},{20,24},{24,28},{29,1},{... | collective-permute-start | bytes 2359304 | tf_op jit(solution)/shard_map/while/body/eval_jaxpr/ppermute | solution.py:20
  300.3 19.0 %collective-permute-start.2 = (bf16[2,2,128,768]{2,3,1,0:T(8,128)(2,1)S(1)}, bf16[2,2,128,768]{2,3,1,0:T(8,128)(2,1)S(1)}, u32[]{:S(2)}, u32[]{:S(2)}) collective-permute-start(bf16[2,2,128,768]{2,3,1,0:T(8,128)(2,1)S(1)} %fusion.222), channel_id=1, source_target_pairs={{28,0},{0,4},{4,8},{8,12},{12,16},{16,20},{20,24},{24,28},{29,1},{... | collective-permute-start | bytes 2359304 | tf_op jit(solution)/shard_map/while/body/eval_jaxpr/ppermute | solution.py:20
  302.1 17.1 %copy-start.56 = (f32[12,32]{1,0:T(8,128)}, f32[12,32]{1,0:T(8,128)S(1)}, u32[]{:S(2)}) copy-start(f32[12,32]{1,0:T(8,128)S(1)} %fusion.224) | copy-start | bytes 4612 | tf_op jit(solution)/shard_map/while
  319.2 17.9 %collective-permute-start.1 = (bf16[2,2,128,768]{2,3,1,0:T(8,128)(2,1)}, bf16[2,2,128,768]{2,3,1,0:T(8,128)(2,1)S(1)}, u32[]{:S(2)}, u32[]{:S(2)}) collective-permute-start(bf16[2,2,128,768]{2,3,1,0:T(8,128)(2,1)} %get-tuple-element.1127), channel_id=1, source_target_pairs={{28,0},{0,4},{4,8},{8,12},{12,16},{16,20},{20,24},{24,28},{29,1},{... | collective-permute-start | bytes 2359304 | tf_op jit(solution)/shard_map/while/body/eval_jaxpr/ppermute | solution.py:20
  339.6 21.1 %collective-permute-start.2 = (bf16[2,2,128,768]{2,3,1,0:T(8,128)(2,1)S(1)}, bf16[2,2,128,768]{2,3,1,0:T(8,128)(2,1)S(1)}, u32[]{:S(2)}, u32[]{:S(2)}) collective-permute-start(bf16[2,2,128,768]{2,3,1,0:T(8,128)(2,1)S(1)} %fusion.222), channel_id=1, source_target_pairs={{28,0},{0,4},{4,8},{8,12},{12,16},{16,20},{20,24},{24,28},{29,1},{... | collective-permute-start | bytes 2359304 | tf_op jit(solution)/shard_map/while/body/eval_jaxpr/ppermute | solution.py:20
  341.5 19.3 %copy-start.56 = (f32[12,32]{1,0:T(8,128)}, f32[12,32]{1,0:T(8,128)S(1)}, u32[]{:S(2)}) copy-start(f32[12,32]{1,0:T(8,128)S(1)} %fusion.224) | copy-start | bytes 4612 | tf_op jit(solution)/shard_map/while
  360.8 20.1 %collective-permute-start.1 = (bf16[2,2,128,768]{2,3,1,0:T(8,128)(2,1)}, bf16[2,2,128,768]{2,3,1,0:T(8,128)(2,1)S(1)}, u32[]{:S(2)}, u32[]{:S(2)}) collective-permute-start(bf16[2,2,128,768]{2,3,1,0:T(8,128)(2,1)} %get-tuple-element.1127), channel_id=1, source_target_pairs={{28,0},{0,4},{4,8},{8,12},{12,16},{16,20},{20,24},{24,28},{29,1},{... | collective-permute-start | bytes 2359304 | tf_op jit(solution)/shard_map/while/body/eval_jaxpr/ppermute | solution.py:20
  383.3 23.0 %collective-permute-start.2 = (bf16[2,2,128,768]{2,3,1,0:T(8,128)(2,1)S(1)}, bf16[2,2,128,768]{2,3,1,0:T(8,128)(2,1)S(1)}, u32[]{:S(2)}, u32[]{:S(2)}) collective-permute-start(bf16[2,2,128,768]{2,3,1,0:T(8,128)(2,1)S(1)} %fusion.222), channel_id=1, source_target_pairs={{28,0},{0,4},{4,8},{8,12},{12,16},{16,20},{20,24},{24,28},{29,1},{... | collective-permute-start | bytes 2359304 | tf_op jit(solution)/shard_map/while/body/eval_jaxpr/ppermute | solution.py:20
  385.2 21.1 %copy-start.56 = (f32[12,32]{1,0:T(8,128)}, f32[12,32]{1,0:T(8,128)S(1)}, u32[]{:S(2)}) copy-start(f32[12,32]{1,0:T(8,128)S(1)} %fusion.224) | copy-start | bytes 4612 | tf_op jit(solution)/shard_map/while
  406.3 22.0 %collective-permute-start.1 = (bf16[2,2,128,768]{2,3,1,0:T(8,128)(2,1)}, bf16[2,2,128,768]{2,3,1,0:T(8,128)(2,1)S(1)}, u32[]{:S(2)}, u32[]{:S(2)}) collective-permute-start(bf16[2,2,128,768]{2,3,1,0:T(8,128)(2,1)} %get-tuple-element.1127), channel_id=1, source_target_pairs={{28,0},{0,4},{4,8},{8,12},{12,16},{16,20},{20,24},{24,28},{29,1},{... | collective-permute-start | bytes 2359304 | tf_op jit(solution)/shard_map/while/body/eval_jaxpr/ppermute | solution.py:20
  430.8 21.0 %collective-permute-start.2 = (bf16[2,2,128,768]{2,3,1,0:T(8,128)(2,1)S(1)}, bf16[2,2,128,768]{2,3,1,0:T(8,128)(2,1)S(1)}, u32[]{:S(2)}, u32[]{:S(2)}) collective-permute-start(bf16[2,2,128,768]{2,3,1,0:T(8,128)(2,1)S(1)} %fusion.222), channel_id=1, source_target_pairs={{28,0},{0,4},{4,8},{8,12},{12,16},{16,20},{20,24},{24,28},{29,1},{... | collective-permute-start | bytes 2359304 | tf_op jit(solution)/shard_map/while/body/eval_jaxpr/ppermute | solution.py:20
  432.7 19.1 %copy-start.56 = (f32[12,32]{1,0:T(8,128)}, f32[12,32]{1,0:T(8,128)S(1)}, u32[]{:S(2)}) copy-start(f32[12,32]{1,0:T(8,128)S(1)} %fusion.224) | copy-start | bytes 4612 | tf_op jit(solution)/shard_map/while
  451.8 22.6 %collective-permute-start.1 = (bf16[2,2,128,768]{2,3,1,0:T(8,128)(2,1)}, bf16[2,2,128,768]{2,3,1,0:T(8,128)(2,1)S(1)}, u32[]{:S(2)}, u32[]{:S(2)}) collective-permute-start(bf16[2,2,128,768]{2,3,1,0:T(8,128)(2,1)} %get-tuple-element.1127), channel_id=1, source_target_pairs={{28,0},{0,4},{4,8},{8,12},{12,16},{16,20},{20,24},{24,28},{29,1},{... | collective-permute-start | bytes 2359304 | tf_op jit(solution)/shard_map/while/body/eval_jaxpr/ppermute | solution.py:20
  476.8 19.3 %collective-permute-start.2 = (bf16[2,2,128,768]{2,3,1,0:T(8,128)(2,1)S(1)}, bf16[2,2,128,768]{2,3,1,0:T(8,128)(2,1)S(1)}, u32[]{:S(2)}, u32[]{:S(2)}) collective-permute-start(bf16[2,2,128,768]{2,3,1,0:T(8,128)(2,1)S(1)} %fusion.222), channel_id=1, source_target_pairs={{28,0},{0,4},{4,8},{8,12},{12,16},{16,20},{20,24},{24,28},{29,1},{... | collective-permute-start | bytes 2359304 | tf_op jit(solution)/shard_map/while/body/eval_jaxpr/ppermute | solution.py:20
  478.7 17.4 %copy-start.56 = (f32[12,32]{1,0:T(8,128)}, f32[12,32]{1,0:T(8,128)S(1)}, u32[]{:S(2)}) copy-start(f32[12,32]{1,0:T(8,128)S(1)} %fusion.224) | copy-start | bytes 4612 | tf_op jit(solution)/shard_map/while
  496.1 20.8 %collective-permute-start.1 = (bf16[2,2,128,768]{2,3,1,0:T(8,128)(2,1)}, bf16[2,2,128,768]{2,3,1,0:T(8,128)(2,1)S(1)}, u32[]{:S(2)}, u32[]{:S(2)}) collective-permute-start(bf16[2,2,128,768]{2,3,1,0:T(8,128)(2,1)} %get-tuple-element.1127), channel_id=1, source_target_pairs={{28,0},{0,4},{4,8},{8,12},{12,16},{16,20},{20,24},{24,28},{29,1},{... | collective-permute-start | bytes 2359304 | tf_op jit(solution)/shard_map/while/body/eval_jaxpr/ppermute | solution.py:20
  519.4 17.4 %collective-permute-start.2 = (bf16[2,2,128,768]{2,3,1,0:T(8,128)(2,1)S(1)}, bf16[2,2,128,768]{2,3,1,0:T(8,128)(2,1)S(1)}, u32[]{:S(2)}, u32[]{:S(2)}) collective-permute-start(bf16[2,2,128,768]{2,3,1,0:T(8,128)(2,1)S(1)} %fusion.222), channel_id=1, source_target_pairs={{28,0},{0,4},{4,8},{8,12},{12,16},{16,20},{20,24},{24,28},{29,1},{... | collective-permute-start | bytes 2359304 | tf_op jit(solution)/shard_map/while/body/eval_jaxpr/ppermute | solution.py:20
  521.3 15.6 %copy-start.56 = (f32[12,32]{1,0:T(8,128)}, f32[12,32]{1,0:T(8,128)S(1)}, u32[]{:S(2)}) copy-start(f32[12,32]{1,0:T(8,128)S(1)} %fusion.224) | copy-start | bytes 4612 | tf_op jit(solution)/shard_map/while
  536.9 19.0 %collective-permute-start.1 = (bf16[2,2,128,768]{2,3,1,0:T(8,128)(2,1)}, bf16[2,2,128,768]{2,3,1,0:T(8,128)(2,1)S(1)}, u32[]{:S(2)}, u32[]{:S(2)}) collective-permute-start(bf16[2,2,128,768]{2,3,1,0:T(8,128)(2,1)} %get-tuple-element.1127), channel_id=1, source_target_pairs={{28,0},{0,4},{4,8},{8,12},{12,16},{16,20},{20,24},{24,28},{29,1},{... | collective-permute-start | bytes 2359304 | tf_op jit(solution)/shard_map/while/body/eval_jaxpr/ppermute | solution.py:20
  558.3 14.7 %collective-permute-start.2 = (bf16[2,2,128,768]{2,3,1,0:T(8,128)(2,1)S(1)}, bf16[2,2,128,768]{2,3,1,0:T(8,128)(2,1)S(1)}, u32[]{:S(2)}, u32[]{:S(2)}) collective-permute-start(bf16[2,2,128,768]{2,3,1,0:T(8,128)(2,1)S(1)} %fusion.222), channel_id=1, source_target_pairs={{28,0},{0,4},{4,8},{8,12},{12,16},{16,20},{20,24},{24,28},{29,1},{... | collective-permute-start | bytes 2359304 | tf_op jit(solution)/shard_map/while/body/eval_jaxpr/ppermute | solution.py:20
  560.2 12.9 %copy-start.56 = (f32[12,32]{1,0:T(8,128)}, f32[12,32]{1,0:T(8,128)S(1)}, u32[]{:S(2)}) copy-start(f32[12,32]{1,0:T(8,128)S(1)} %fusion.224) | copy-start | bytes 4612 | tf_op jit(solution)/shard_map/while
  575.7 52.0 %reduce-scatter.11.cloned.1.call-start = ((), (), s32[]{:S(2)}) async-start(), calls=%async_computation.14 | async-start | bytes 1474560 | tf_op jit(solution)/shard_map/reduce_scatter | solution.py:351
  577.3 79.3 %reduce-scatter.7.cloned.1.call-start = ((), (), s32[]{:S(2)}) async-start(), calls=%async_computation.12 | async-start | bytes 1474560 | tf_op jit(solution)/shard_map/reduce_scatter | solution.py:345
  579.4 127.6 %reduce-scatter.17.cloned.1.call-start = ((), (), s32[]{:S(2)}) async-start(), calls=%async_computation.17 | async-start | bytes 5898240 | tf_op jit(solution)/shard_map/reduce_scatter | solution.py:366
  583.2 174.2 %reduce-scatter.15.cloned.1.call-start = ((), (), s32[]{:S(2)}) async-start(), calls=%async_computation.16 | async-start | bytes 5898240 | tf_op jit(solution)/shard_map/reduce_scatter | solution.py:363
  (103 other events, 238.5 us)
Sparse Core Ops, SparseCore 0:
  9.6 20.2 all-gather.10
  31.5 17.4 all-gather.6
  50.5 17.4 all-gather.8
  69.4 17.4 all-gather.12
  88.4 37.4 all-gather.14
  127.3 37.4 all-gather.16
  268.5 27.3 reduce-scatter.12
  575.8 23.3 reduce-scatter.8
  601.8 25.8 reduce-scatter.10
  630.8 25.7 reduce-scatter.6
  659.1 47.8 reduce-scatter.16
  709.6 47.8 reduce-scatter.14
